TPU v7x, 32 devices: a whole 2x2x4 slice. The times are simulated.
32 devices in a mesh: groups: 2 (over x), tm: 16 (over z, y, core).
Axes of the slice: x: 2, y: 2, z: 4, core: 2. Of those that a mesh axis runs over, the one named last changes fastest.
Arguments:
- frames: float32 [64, 196, 1024], P(('groups', 'tm')), parts along dimension 0, may hold values from -6 to 6
- cotangent: float32 [64, 196, 1024], P(('groups', 'tm')), parts along dimension 0, may hold values from -6 to 6
- reduce_weight: float32 [1024, 256], replicated, may hold values from -0.1875 to 0.1875
- spatial_weight: float32 [2304, 256], replicated, may hold values from -0.125 to 0.125
- expand_weight: float32 [1024, 256], replicated, may hold values from -0.375 to 0.375
- reduce_scale: float32 [256], replicated, may hold values from 0.5 to 2
- reduce_bias: float32 [256], replicated, may hold values from -0.8 to 0.8
- spatial_scale: float32 [256], replicated, may hold values from 0.5 to 2
- spatial_bias: float32 [256], replicated, may hold values from -0.8 to 0.8
- expand_scale: float32 [1024], replicated, may hold values from 0.5 to 2
- expand_bias: float32 [1024], replicated, may hold values from -0.8 to 0.8
Outputs:
- block_out: float32 [64, 196, 1024], P(('groups', 'tm')), parts along dimension 0
- grad_frames: float32 [64, 196, 1024], P(('groups', 'tm')), parts along dimension 0
- grad_reduce: float32 [2048, 256], P(('groups', 'tm')), parts along dimension 0
- grad_spatial: float32 [4608, 256], P(('groups', 'tm')), parts along dimension 0
- grad_expand: float32 [2048, 256], P(('groups', 'tm')), parts along dimension 0
There are 2 independent parts, one for each index of `groups`. A program takes and returns all parts, laid end to end along the dimension named above; an argument that names none is the same for every part. Nothing has to cross between parts.
All inputs are finite; a program needn't handle non-finite values.
Results may differ from a plain program's by a relative error of at most 0.00007.
Values sent between devices are 32-bit elements; how exact they have to be, the bound alone decides.
No kernel may reach another device: no remote copies, remote signals or barrier semaphores. Data moves between devices by JAX's collectives and lax.ppermute only.
A program may use at most 128 MiB of HBM per device.

v0:
```python
import functools
import math

import jax
import jax.numpy as jnp
from jax import lax
from jax.experimental import pallas as pl
from jax.experimental.pallas import tpu as pltpu
from jax.sharding import PartitionSpec as P


F32 = jnp.float32
BF16 = jnp.bfloat16
ROOT = math.sqrt(2.0 / math.pi)
CUBE = 0.044715
NN = (((1,), (0,)), ((), ()))
NT = (((1,), (1,)), ((), ()))


def passed_along(block, axis, distance):
    devices = range(lax.axis_size(axis))
    route = [(i - distance, i) for i in devices if i - distance in devices]
    return lax.ppermute(block, axis, route)


def split(values):
    high = values.astype(BF16)
    low = (values - high.astype(F32)).astype(BF16)
    return high, low


def product(left, right, dims=NN):
    def one(a, b):
        return lax.dot_general(a, b, dims, preferred_element_type=F32)

    return one(left[0], right[0]) + (one(left[0], right[1]) + one(left[1], right[0]))


def gelu_pair(values):
    square = values * values
    turned = jnp.tanh(ROOT * values * (1.0 + CUBE * square))
    half = 0.5 * (1.0 + turned)
    slope = half + (0.5 * ROOT) * values * (1.0 - turned * turned) * (
        1.0 + (3.0 * CUBE) * square
    )
    return values * half, slope


def pick(pair, index):
    return pair[0][index], pair[1][index]


class Sizes:
    def __init__(self, nframes, ncells, channels, middle, shards):
        self.nframes, self.ncells = nframes, ncells
        self.channels, self.middle, self.shards = channels, middle, shards
        self.extent = math.isqrt(ncells)
        self.pitch = 16
        self.rows = self.extent * self.pitch
        self.tall = (self.extent + 2) * self.pitch
        self.folded = channels // 8


def view(array):
    nframes, ncells, channels = array.shape
    turned = array.transpose(1, 0, 2).reshape(ncells, nframes, channels // 128, 128)
    return turned.transpose(0, 2, 1, 3).reshape(-1, 128)


def unview(rows, shape):
    nframes, ncells, channels = shape
    turned = rows.reshape(ncells, channels // 128, nframes, 128).transpose(0, 2, 1, 3)
    return turned.reshape(ncells, nframes, channels).transpose(1, 0, 2)


def tile_rows(sz, t, tile):
    return pl.ds(sz.nframes * tile + t, sz.ncells, stride=sz.nframes * (sz.channels // 128))


def take(sz, ref, t, lo=0, hi=None):
    hi = sz.channels if hi is None else hi
    tiles = [ref[tile_rows(sz, t, j), :] for j in range(lo // 128, hi // 128)]
    return tiles[0] if len(tiles) == 1 else jnp.concatenate(tiles, axis=1)


def put(sz, ref, t, values, lo=0):
    for j in range(values.shape[1] // 128):
        ref[tile_rows(sz, t, lo // 128 + j), :] = values[:, 128 * j : 128 * (j + 1)]


def to_pitch(sz, target, frame, flat):
    for row in range(sz.extent):
        at = 8 + sz.pitch * (row + 1)
        target[frame, at : at + sz.extent, :] = flat[row * sz.extent : (row + 1) * sz.extent]


def to_flat(sz, target, frame, pitched):
    for row in range(sz.extent):
        target[frame, row * sz.extent : (row + 1) * sz.extent, :] = pitched[
            row * sz.pitch : row * sz.pitch + sz.extent
        ]


def slot_source(slot, order):
    bits = len(order)
    return sum(((slot >> (bits - 1 - b)) & 1) * order[b] for b in range(bits))


def write_slots(sz, me, source, outs, order):
    rows = source.shape[0] // sz.shards
    base = sz.shards
    for out in outs:
        count = out.shape[0] // rows
        base -= count
        for k in range(count):
            chunk = jnp.bitwise_xor(me, slot_source(base + k, order))
            out[k * rows : (k + 1) * rows, :] = source[
                pl.ds(pl.multiple_of(chunk * rows, 8), rows), :
            ]


def slot_shapes(sz, total, width):
    rows = total // sz.shards
    counts, left = [], sz.shards
    while left > 1:
        left //= 2
        counts.append(left)
    counts.append(1)
    return [jax.ShapeDtypeStruct((c * rows, width), F32) for c in counts]


def begin_kernel(sz, frames, weight, part):
    f = sz.folded
    w = split(weight[...])
    for t in range(sz.nframes):
        total = product(split(take(sz, frames, t, 2 * f)), pick(w, slice(2 * f, None)))
        if t + 1 < sz.nframes:
            total += product(split(take(sz, frames, t + 1, 0, f)), pick(w, slice(0, f)))
        if t > 0:
            total += product(split(take(sz, frames, t - 1, f, 2 * f)), pick(w, slice(f, 2 * f)))
        part[t] = total


def middle_kernel(
    sz, part, from_next, from_prev, frames, cotangent, w1, w2, w3,
    rs, rb, ss, sb, es, eb, *refs
):
    block_out, residual, padded_one, padded_grad, slope_one, flat, high, low = refs
    f, n = sz.folded, sz.nframes
    padded_one[...] = jnp.zeros_like(padded_one)
    padded_grad[...] = jnp.zeros_like(padded_grad)
    for t in range(n):
        pre = part[t]
        if t + 1 == n:
            pre += product(split(from_next[0]), split(w1[:f, :]))
        if t == 0:
            pre += product(split(from_prev[0]), split(w1[f : 2 * f, :]))
        hidden, slope = gelu_pair(rs[...] * pre + rb[...])
        slope_one[t] = slope * rs[...]
        to_pitch(sz, padded_one, t, hidden)
    for c in range(3):
        h, l = split(padded_one[:, 7 + c : 7 + c + sz.tall, :])
        high[c], low[c] = h, l
    total = jnp.zeros((n * sz.rows, sz.middle), F32)
    for r in range(3):
        for c in range(3):
            tap = 3 * r + c
            cut = slice(sz.pitch * r, sz.pitch * r + sz.rows)
            left = (
                high[c, :, cut, :].reshape(n * sz.rows, sz.middle),
                low[c, :, cut, :].reshape(n * sz.rows, sz.middle),
            )
            total += product(left, split(w2[tap * sz.middle : (tap + 1) * sz.middle, :]))
    hidden_two, slope_two = gelu_pair(ss[...] * total + sb[...])
    slope_two = slope_two * ss[...]
    w = split(w3[...])
    for t in range(n):
        to_flat(sz, flat, t, hidden_two[t * sz.rows : (t + 1) * sz.rows])
    for t in range(n):
        pre = es[...] * product(split(flat[t]), w, NT) + eb[...] + take(sz, frames, t)
        block, slope = gelu_pair(pre)
        put(sz, block_out, t, block)
        residual[t] = take(sz, cotangent, t) * slope
    for t in range(n):
        grad = residual[t] * es[...]
        back = product(split(grad), w)
        for row in range(sz.extent):
            at = 8 + sz.pitch * (row + 1)
            lo = t * sz.rows + row * sz.pitch
            padded_grad[t, at : at + sz.extent, :] = (
                back[row * sz.extent : (row + 1) * sz.extent]
                * slope_two[lo : lo + sz.extent]
            )


def expand_kernel(sz, order, me_ref, residual, flat, es, *refs):
    outs, (whole,) = refs[:-1], refs[-1:]
    pairs = [split(flat[t]) for t in range(sz.nframes)]
    step = 256
    for lo in range(0, sz.channels, step):
        total = jnp.zeros((step, sz.middle), F32)
        for t in range(sz.nframes):
            grad = residual[t, :, lo : lo + step] * es[:, lo : lo + step]
            total += product(split(grad.T), pairs[t])
        whole[lo : lo + step, :] = total
    if order is None:
        outs[0][...] = whole[...]
    else:
        write_slots(sz, me_ref[0], whole, outs, order)


def shifted_grads(sz, padded_grad, c):
    return split(padded_grad[:, 9 - c : 9 - c + sz.tall, :])


def spatial_kernel(sz, order, me_ref, padded_one, padded_grad, *refs):
    outs, (whole,) = refs[:-1], refs[-1:]
    n = sz.nframes
    at = 8 + sz.pitch
    turned = split(
        padded_one[:, at : at + sz.rows, :].reshape(n * sz.rows, sz.middle).T
    )
    for c in range(3):
        pair = shifted_grads(sz, padded_grad, c)
        for r in range(3):
            tap = 3 * r + c
            cut = slice(sz.pitch * (2 - r), sz.pitch * (2 - r) + sz.rows)
            right = tuple(x[:, cut, :].reshape(n * sz.rows, sz.middle) for x in pair)
            whole[tap * sz.middle : (tap + 1) * sz.middle, :] = product(turned, right)
    if order is None:
        outs[0][...] = whole[...]
    else:
        write_slots(sz, me_ref[0], whole, outs, order)


def reduce_kernel(
    sz, order, me_ref, padded_grad, slope_one, w2, w1, frames, from_next, from_prev, *refs
):
    reduce_grad, ahead, behind = refs[:3]
    outs, (whole,) = refs[3:-1], refs[-1:]
    n, f = sz.nframes, sz.folded
    total = jnp.zeros((n * sz.rows, sz.middle), F32)
    for c in range(3):
        pair = shifted_grads(sz, padded_grad, c)
        for r in range(3):
            tap = 3 * r + c
            cut = slice(sz.pitch * (2 - r), sz.pitch * (2 - r) + sz.rows)
            left = tuple(x[:, cut, :].reshape(n * sz.rows, sz.middle) for x in pair)
            total += product(left, split(w2[tap * sz.middle : (tap + 1) * sz.middle, :]), NT)
    for t in range(n):
        for row in range(sz.extent):
            lo = t * sz.rows + row * sz.pitch
            cut = slice(row * sz.extent, (row + 1) * sz.extent)
            reduce_grad[t, cut, :] = total[lo : lo + sz.extent] * slope_one[t, cut, :]
    ahead[0] = product(split(reduce_grad[n - 1]), split(w1[:f, :]), NT)
    behind[0] = product(split(reduce_grad[0]), split(w1[f : 2 * f, :]), NT)
    pairs = [split(reduce_grad[t]) for t in range(n)]
    for lo in range(0, sz.channels, f):
        total = jnp.zeros((f, sz.middle), F32)
        for t in range(n):
            if lo == 0:
                block = take(sz, frames, t + 1, 0, f) if t + 1 < n else from_next[0]
            elif lo == f:
                block = take(sz, frames, t - 1, f, 2 * f) if t > 0 else from_prev[0]
            else:
                block = take(sz, frames, t, lo, lo + f)
            total += product(split(block.T), pairs[t])
        whole[lo : lo + f, :] = total
    if order is None:
        outs[0][...] = whole[...]
    else:
        write_slots(sz, me_ref[0], whole, outs, order)


def end_kernel(sz, reduce_grad, w1, residual, before, after, grad_frames):
    n, f = sz.nframes, sz.folded
    w = split(w1[...])
    for t in range(n):
        back = product(split(reduce_grad[t]), w, NT)
        put(sz, grad_frames, t, residual[t, :, 2 * f :] + back[:, 2 * f :], 2 * f)
        if t + 1 < n:
            put(sz, grad_frames, t + 1, residual[t + 1, :, :f] + back[:, :f])
        if t > 0:
            put(
                sz, grad_frames, t - 1,
                residual[t - 1, :, f : 2 * f] + back[:, f : 2 * f], f,
            )
    put(sz, grad_frames, 0, residual[0, :, :f] + before[0])
    put(sz, grad_frames, n - 1, residual[n - 1, :, f : 2 * f] + after[0], f)


VM = pl.BlockSpec(memory_space=pltpu.VMEM)
SM = pl.BlockSpec(memory_space=pltpu.SMEM)


def call(kernel, outs, ins, scratch=(), scalar=False, flops=0):
    specs = [VM] * len(ins)
    if scalar:
        specs[0] = SM
    moved = sum(4 * math.prod(x.shape) for x in list(ins) + list(outs))
    return pl.pallas_call(
        kernel,
        out_shape=list(outs),
        in_specs=specs,
        out_specs=[VM] * len(outs),
        scratch_shapes=list(scratch),
        compiler_params=pltpu.CompilerParams(vmem_limit_bytes=58 * 1024 * 1024),
        cost_estimate=pl.CostEstimate(flops=flops, bytes_accessed=moved, transcendentals=0),
    )(*ins)


def scatter_sum(sz, pieces, order):
    shards = sz.shards
    if order is None:
        return lax.psum_scatter(pieces[0], "tm", scatter_dimension=0, tiled=True)
    arrived = []
    for stage, piece in enumerate(pieces[:-1]):
        rows = piece.shape[0]
        for block in arrived:
            piece = piece + block[rows : 2 * rows]
        route = [(i, i ^ order[stage]) for i in range(shards)]
        arrived.append(lax.ppermute(piece, "tm", route))
    total = pieces[-1]
    for block in arrived:
        total = total + block[: total.shape[0]]
    return total


def local(
    frames,
    cotangent,
    reduce_weight,
    spatial_weight,
    expand_weight,
    reduce_scale,
    reduce_bias,
    spatial_scale,
    spatial_bias,
    expand_scale,
    expand_bias,
):
    nframes, ncells, channels = frames.shape
    middle = reduce_weight.shape[1]
    shards = lax.axis_size("tm")
    sz = Sizes(nframes, ncells, channels, middle, shards)
    f = sz.folded

    def order_of(total):
        if shards & (shards - 1) or shards == 1 or total % (8 * shards):
            return None
        return [1 << b for b in range(shards.bit_length() - 1)]

    def grads(total):
        if order_of(total) is None:
            return [jax.ShapeDtypeStruct((total, middle), F32)]
        return slot_shapes(sz, total, middle)

    def full(*shape):
        return jax.ShapeDtypeStruct(shape, F32)

    me = lax.axis_index("tm").astype(jnp.int32).reshape(1)
    work = 6 * nframes * ncells * middle
    from_next = passed_along(frames[:1, :, :f], "tm", -1)
    from_prev = passed_along(frames[-1:, :, f : 2 * f], "tm", 1)
    rs, rb, ss, sb, es, eb = [
        x.reshape(1, -1)
        for x in (reduce_scale, reduce_bias, spatial_scale, spatial_bias, expand_scale, expand_bias)
    ]
    frame_rows = view(frames)
    lines = full(*frame_rows.shape)
    (part,) = call(
        functools.partial(begin_kernel, sz),
        [full(nframes, ncells, middle)],
        [frame_rows, reduce_weight],
        flops=work * channels,
    )
    block_out, residual, padded_one, padded_grad, slope_one, flat = call(
        functools.partial(middle_kernel, sz),
        [
            lines,
            full(nframes, ncells, channels),
            full(nframes, sz.tall + 16, middle),
            full(nframes, sz.tall + 16, middle),
            full(nframes, ncells, middle),
            full(nframes, ncells, middle),
        ],
        [part, from_next, from_prev, frame_rows, view(cotangent), reduce_weight, spatial_weight,
         expand_weight, rs, rb, ss, sb, es, eb],
        [
            pltpu.VMEM((3, nframes, sz.tall, middle), BF16),
            pltpu.VMEM((3, nframes, sz.tall, middle), BF16),
        ],
        flops=work * (9 * middle + 2 * channels),
    )
    spatial_order, channel_order = order_of(9 * middle), order_of(channels)
    spatial_pieces = call(
        functools.partial(spatial_kernel, sz, spatial_order),
        grads(9 * middle),
        [me, padded_one, padded_grad],
        [pltpu.VMEM((9 * middle, middle), F32)],
        scalar=True,
        flops=work * 9 * middle,
    )
    grad_spatial = scatter_sum(sz, spatial_pieces, spatial_order)
    expand_pieces = call(
        functools.partial(expand_kernel, sz, channel_order),
        grads(channels),
        [me, residual, flat, es],
        [pltpu.VMEM((channels, middle), F32)],
        scalar=True,
        flops=work * channels,
    )
    grad_expand = scatter_sum(sz, expand_pieces, channel_order)
    reduce_grad, ahead, behind, *reduce_pieces = call(
        functools.partial(reduce_kernel, sz, channel_order),
        [full(nframes, ncells, middle), full(1, ncells, f), full(1, ncells, f)] + grads(channels),
        [me, padded_grad, slope_one, spatial_weight, reduce_weight, frame_rows, from_next, from_prev],
        [pltpu.VMEM((channels, middle), F32)],
        scalar=True,
        flops=work * (9 * middle + channels),
    )
    before = passed_along(ahead, "tm", 1)
    after = passed_along(behind, "tm", -1)
    grad_reduce = scatter_sum(sz, reduce_pieces, channel_order)
    (grad_frames,) = call(
        functools.partial(end_kernel, sz),
        [lines],
        [reduce_grad, reduce_weight, residual, before, after],
        flops=work * channels,
    )
    return (
        unview(block_out, frames.shape),
        unview(grad_frames, frames.shape),
        grad_reduce,
        grad_spatial,
        grad_expand,
    )


def solution(mesh):
    return jax.shard_map(
        local,
        mesh=mesh,
        in_specs=(
            P(("groups", "tm"), None, None),
            P(("groups", "tm"), None, None),
            P(),
            P(),
            P(),
            P(),
            P(),
            P(),
            P(),
            P(),
            P(),
        ),
        out_specs=(
            P(("groups", "tm"), None, None),
            P(("groups", "tm"), None, None),
            P(("groups", "tm"), None),
            P(("groups", "tm"), None),
            P(("groups", "tm"), None),
        ),
        check_vma=False,
    )
```

profile of v0, /device:TPU:0, one launch (start us, length us, event | category | flops | bytes accessed | tf_op | source)
XLA Modules:
  0.0 105.5 jit_solution(1508691799691951523)
XLA Ops:
  3.2 3.0 %collective-permute-start.1 = (f32[1,196,128]{2,1,0:T(8,128)S(1)}, f32[1,196,128]{2,1,0:T(8,128)S(1)}, u32[]{:S(2)}, u32[]{:S(2)}) collective-permute-start(f32[1,196,128]{2,1,0:T(8,128)S(1)} %copy.21), channel_id=1, source_target_pairs={{0,1},{1,2},{2,3},{3,4},{4,5},{5,6},{6,7},{7,8},{8,9},{9,10},{10,1... | collective-permute-start | bytes 301064 | tf_op jit(solution)/shard_map/ppermute | solution.py:23
  6.2 3.5 %shard_map.146.part = f32[2,196,256]{2,1,0:T(8,128)} custom-call(f32[3136,128]{1,0:T(8,128)} %bitcast.35, f32[1024,256]{1,0:T(8,128)} %w1.5), custom_call_target="tpu_custom_call" | custom-call | flops 616562688 | bytes 3055616 | tf_op jit(solution)/shard_map/pallas_call | solution.py:301
  10.4 12.4 %shard_map.147 = (f32[3136,128]{1,0:T(8,128)}, f32[2,196,1024]{2,1,0:T(8,128)}, f32[2,272,256]{2,1,0:T(8,128)}, f32[2,272,256]{2,1,0:T(8,128)}, f32[2,196,256]{2,1,0:T(8,128)}, /*index=5*/f32[2,196,256]{2,1,0:T(8,128)}) custom-call(f32[2,196,256]{2,1,0:T(8,128)} %shard_map.146.part, f32[1,196,128]{2,1,0:T(8,128)} %copy-done.14, f32[1,196,128]{2,1,0:T(8,128)} %copy-done.15, ...), custom_call_target="tpu_custom_call" | custom-call | flops 2620391424 | bytes 13410304 | tf_op jit(solution)/shard_map/pallas_call | solution.py:301
  22.8 4.8 %shard_map.150 = (f32[1152,256]{1,0:T(8,128)}, f32[576,256]{1,0:T(8,128)}, f32[288,256]{1,0:T(8,128)}, f32[144,256]{1,0:T(8,128)}, f32[144,256]{1,0:T(8,128)}) custom-call(s32[1]{0:T(128)} %bitcast.18.me_ref, f32[2,272,256]{2,1,0:T(8,128)} %get-tuple-element.41.padded_one, f32[2,272,256]{2,1,0:T(8,128)} %get-tuple-element.30.padded_grad), custom_call_target="tpu_custom_call" | custom-call | flops 1387266048 | bytes 3473412 | tf_op jit(solution)/shard_map/pallas_call | solution.py:301
  27.5 2.6 %collective-permute-start.8 = (f32[1152,256]{1,0:T(8,128)}, f32[1152,256]{1,0:T(8,128)S(1)}, u32[]{:S(2)}, u32[]{:S(2)}) collective-permute-start(f32[1152,256]{1,0:T(8,128)} %get-tuple-element.43), channel_id=1, source_target_pairs={{0,1},{1,0},{2,3},{3,2},{4,5},{5,4},{6,7},{7,6},{8,9},{9,8},{10,11... | collective-permute-start | bytes 3538952 | tf_op jit(solution)/shard_map/ppermute | solution.py:322
  30.2 3.7 %shard_map.151 = (f32[512,256]{1,0:T(8,128)}, f32[256,256]{1,0:T(8,128)}, f32[128,256]{1,0:T(8,128)}, f32[64,256]{1,0:T(8,128)}, f32[64,256]{1,0:T(8,128)}) custom-call(s32[1]{0:T(128)} %bitcast.18.me_ref, f32[2,196,1024]{2,1,0:T(8,128)} %get-tuple-element.33.residual, f32[2,196,256]{2,1,0:T(8,128)} %get-tuple-element.47.flat, f32[1,1024]{1,0:T(1,128)} %bitcast.42), custom_call_target="tpu_custom_call" | custom-call | flops 616562688 | bytes 3059716 | tf_op jit(solution)/shard_map/pallas_call | solution.py:301
  33.9 8.8 %shard_map.148 = (f32[2,196,256]{2,1,0:T(8,128)}, f32[1,196,128]{2,1,0:T(8,128)}, f32[1,196,128]{2,1,0:T(8,128)}, f32[512,256]{1,0:T(8,128)}, f32[256,256]{1,0:T...) custom-call(s32[1]{0:T(128)} %bitcast.18.me_ref, ...), custom_call_target="tpu_custom_call" | custom-call | flops 2003828736 | bytes 7823364 | tf_op jit(solution)/shard_map/pallas_call | solution.py:301
  43.1 1.9 %collective-permute-start.2 = (f32[1,196,128]{2,1,0:T(8,128)}, f32[1,196,128]{2,1,0:T(8,128)S(1)}, u32[]{:S(2)}, u32[]{:S(2)}) collective-permute-start(f32[1,196,128]{2,1,0:T(8,128)} %get-tuple-element.34), channel_id=1, source_target_pairs={{0,1},{1,2},{2,3},{3,4},{4,5},{5,6},{6,7},{7,8},{8,9},{9,10},{10,1... | collective-permute-start | bytes 301064 | tf_op jit(solution)/shard_map/ppermute | solution.py:23
  45.1 1.3 %collective-permute-start.3 = (f32[1,196,128]{2,1,0:T(8,128)}, f32[1,196,128]{2,1,0:T(8,128)S(1)}, u32[]{:S(2)}, u32[]{:S(2)}) collective-permute-start(f32[1,196,128]{2,1,0:T(8,128)} %get-tuple-element.35), channel_id=1, source_target_pairs={{1,0},{2,1},{3,2},{4,3},{5,4},{6,5},{7,6},{8,7},{9,8},{10,9},{11,1... | collective-permute-start | bytes 301064 | tf_op jit(solution)/shard_map/ppermute | solution.py:23
  46.4 4.0 %collective-permute-done.3.after = f32[1,196,128]{2,1,0:T(8,128)S(1)} collective-permute-done((f32[1,196,128]{2,1,0:T(8,128)}, f32[1,196,128]{2,1,0:T(8,128)S(1)}, u32[]{:S(2)}, u32[]{:S(2)}) %collective-permute-start.3) | collective-permute-done | bytes 100384 | tf_op jit(solution)/shard_map/ppermute | solution.py:23
  51.1 4.6 %shard_map.149 = f32[3136,128]{1,0:T(8,128)} custom-call(f32[2,196,256]{2,1,0:T(8,128)} %get-tuple-element.32.reduce_grad, f32[1024,256]{1,0:T(8,128)} %w1.5, f32[2,196,1024]{2,1,0:T(8,128)} %get-tuple-element.33.residual, f32[1,196,128]{2,1,0:T(8,128)} %copy-done.8, f32[1,196,128]{2,1,0:T(8,128)} %copy-done.9), custom_call_target="tpu_custom_call" | custom-call | flops 616562688 | bytes 4861952 | tf_op jit(solution)/shard_map/pallas_call | solution.py:301
  55.8 3.2 %collective-permute-start.13 = (f32[256,256]{1,0:T(8,128)S(1)}, f32[256,256]{1,0:T(8,128)S(1)}, u32[]{:S(2)}, u32[]{:S(2)}) collective-permute-start(f32[256,256]{1,0:T(8,128)S(1)} %slice_add_fusion.3), channel_id=1, source_target_pairs={{0,2},{1,3},{2,0},{3,1},{4,6},{5,7},{6,4},{7,5},{8,10},{9,11},{10,... | collective-permute-start | bytes 786440 | tf_op jit(solution)/shard_map/ppermute | solution.py:322
  59.3 2.1 %collective-permute-start.9 = (f32[576,256]{1,0:T(8,128)S(1)}, f32[576,256]{1,0:T(8,128)S(1)}, u32[]{:S(2)}, u32[]{:S(2)}) collective-permute-start(f32[576,256]{1,0:T(8,128)S(1)} %slice_add_fusion), channel_id=1, source_target_pairs={{0,2},{1,3},{2,0},{3,1},{4,6},{5,7},{6,4},{7,5},{8,10},{9,11},{10,... | collective-permute-start | bytes 1769480 | tf_op jit(solution)/shard_map/ppermute | solution.py:322
  61.3 3.2 %collective-permute-done.13 = f32[256,256]{1,0:T(8,128)S(1)} collective-permute-done((f32[256,256]{1,0:T(8,128)S(1)}, f32[256,256]{1,0:T(8,128)S(1)}, u32[]{:S(2)}, u32[]{:S(2)}) %collective-permute-start.13) | collective-permute-done | bytes 262176 | tf_op jit(solution)/shard_map/ppermute | solution.py:322
  64.6 4.0 %collective-permute-start.14 = (f32[128,256]{1,0:T(8,128)S(1)}, f32[128,256]{1,0:T(8,128)S(1)}, u32[]{:S(2)}, u32[]{:S(2)}) collective-permute-start(f32[128,256]{1,0:T(8,128)S(1)} %slice_add_fusion.11), channel_id=1, source_target_pairs={{0,4},{1,5},{2,6},{3,7},{4,0},{5,1},{6,2},{7,3},{8,12},{9,13},{10,... | collective-permute-start | bytes 393224 | tf_op jit(solution)/shard_map/ppermute | solution.py:322
  68.6 1.6 %collective-permute-done.5 = f32[256,256]{1,0:T(8,128)S(1)} collective-permute-done((f32[256,256]{1,0:T(8,128)S(1)}, f32[256,256]{1,0:T(8,128)S(1)}, u32[]{:S(2)}, u32[]{:S(2)}) %collective-permute-start.5) | collective-permute-done | bytes 262176 | tf_op jit(solution)/shard_map/ppermute | solution.py:322
  70.2 4.0 %collective-permute-start.6 = (f32[128,256]{1,0:T(8,128)S(1)}, f32[128,256]{1,0:T(8,128)S(1)}, u32[]{:S(2)}, u32[]{:S(2)}) collective-permute-start(f32[128,256]{1,0:T(8,128)S(1)} %slice_add_fusion.13), channel_id=1, source_target_pairs={{0,4},{1,5},{2,6},{3,7},{4,0},{5,1},{6,2},{7,3},{8,12},{9,13},{10,... | collective-permute-start | bytes 393224 | tf_op jit(solution)/shard_map/ppermute | solution.py:322
  74.3 3.1 %collective-permute-start.15 = (f32[64,256]{1,0:T(8,128)S(1)}, f32[64,256]{1,0:T(8,128)S(1)}, u32[]{:S(2)}, u32[]{:S(2)}) collective-permute-start(f32[64,256]{1,0:T(8,128)S(1)} %slice_add_fusion.15), channel_id=1, source_target_pairs={{0,8},{1,9},{2,10},{3,11},{4,12},{5,13},{6,14},{7,15},{8,0},{9,1},... | collective-permute-start | bytes 196616 | tf_op jit(solution)/shard_map/ppermute | solution.py:322
  77.4 5.5 %collective-permute-done.9 = f32[576,256]{1,0:T(8,128)S(1)} collective-permute-done((f32[576,256]{1,0:T(8,128)S(1)}, f32[576,256]{1,0:T(8,128)S(1)}, u32[]{:S(2)}, u32[]{:S(2)}) %collective-permute-start.9) | collective-permute-done | bytes 589856 | tf_op jit(solution)/shard_map/ppermute | solution.py:322
  82.9 4.0 %collective-permute-start.10 = (f32[288,256]{1,0:T(8,128)S(1)}, f32[288,256]{1,0:T(8,128)S(1)}, u32[]{:S(2)}, u32[]{:S(2)}) collective-permute-start(f32[288,256]{1,0:T(8,128)S(1)} %slice_add_fusion.1), channel_id=1, source_target_pairs={{0,4},{1,5},{2,6},{3,7},{4,0},{5,1},{6,2},{7,3},{8,12},{9,13},{10,... | collective-permute-start | bytes 884744 | tf_op jit(solution)/shard_map/ppermute | solution.py:322
  86.9 1.7 %collective-permute-start.7 = (f32[64,256]{1,0:T(8,128)S(1)}, f32[64,256]{1,0:T(8,128)S(1)}, u32[]{:S(2)}, u32[]{:S(2)}) collective-permute-start(f32[64,256]{1,0:T(8,128)S(1)} %slice_add_fusion.21), channel_id=1, source_target_pairs={{0,8},{1,9},{2,10},{3,11},{4,12},{5,13},{6,14},{7,15},{8,0},{9,1},... | collective-permute-start | bytes 196616 | tf_op jit(solution)/shard_map/ppermute | solution.py:322
  89.3 6.4 %collective-permute-done.10 = f32[288,256]{1,0:T(8,128)S(1)} collective-permute-done((f32[288,256]{1,0:T(8,128)S(1)}, f32[288,256]{1,0:T(8,128)S(1)}, u32[]{:S(2)}, u32[]{:S(2)}) %collective-permute-start.10) | collective-permute-done | bytes 294944 | tf_op jit(solution)/shard_map/ppermute | solution.py:322
  95.8 2.1 %collective-permute-start.11 = (f32[144,256]{1,0:T(8,128)S(1)}, f32[144,256]{1,0:T(8,128)S(1)}, u32[]{:S(2)}, u32[]{:S(2)}) collective-permute-start(f32[144,256]{1,0:T(8,128)S(1)} %slice_add_fusion.5), channel_id=1, source_target_pairs={{0,8},{1,9},{2,10},{3,11},{4,12},{5,13},{6,14},{7,15},{8,0},{9,1},... | collective-permute-start | bytes 442376 | tf_op jit(solution)/shard_map/ppermute | solution.py:322
  98.6 6.3 %collective-permute-done.11 = f32[144,256]{1,0:T(8,128)S(1)} collective-permute-done((f32[144,256]{1,0:T(8,128)S(1)}, f32[144,256]{1,0:T(8,128)S(1)}, u32[]{:S(2)}, u32[]{:S(2)}) %collective-permute-start.11) | collective-permute-done | bytes 147488 | tf_op jit(solution)/shard_map/ppermute | solution.py:322
  (61 shorter events, 6.9 us)
Async XLA Ops:
  1.9 7.9 %collective-permute-start = (f32[1,196,128]{2,1,0:T(8,128)S(1)}, f32[1,196,128]{2,1,0:T(8,128)S(1)}, u32[]{:S(2)}, u32[]{:S(2)}) collective-permute-start(f32[1,196,128]{2,1,0:T(8,128)S(1)} %copy.20), channel_id=1, source_target_pairs={{1,0},{2,1},{3,2},{4,3},{5,4},{6,5},{7,6},{8,7},{9,8},{10,9},{11,1... | collective-permute-start | bytes 301064 | tf_op jit(solution)/shard_map/ppermute | solution.py:23
  3.2 6.6 %collective-permute-start.1 = (f32[1,196,128]{2,1,0:T(8,128)S(1)}, f32[1,196,128]{2,1,0:T(8,128)S(1)}, u32[]{:S(2)}, u32[]{:S(2)}) collective-permute-start(f32[1,196,128]{2,1,0:T(8,128)S(1)} %copy.21), channel_id=1, source_target_pairs={{0,1},{1,2},{2,3},{3,4},{4,5},{5,6},{6,7},{7,8},{8,9},{9,10},{10,1... | collective-permute-start | bytes 301064 | tf_op jit(solution)/shard_map/ppermute | solution.py:23
  27.5 31.6 %collective-permute-start.8 = (f32[1152,256]{1,0:T(8,128)}, f32[1152,256]{1,0:T(8,128)S(1)}, u32[]{:S(2)}, u32[]{:S(2)}) collective-permute-start(f32[1152,256]{1,0:T(8,128)} %get-tuple-element.43), channel_id=1, source_target_pairs={{0,1},{1,0},{2,3},{3,2},{4,5},{5,4},{6,7},{7,6},{8,9},{9,8},{10,11... | collective-permute-start | bytes 3538952 | tf_op jit(solution)/shard_map/ppermute | solution.py:322
  33.9 21.8 %collective-permute-start.12 = (f32[512,256]{1,0:T(8,128)}, f32[512,256]{1,0:T(8,128)S(1)}, u32[]{:S(2)}, u32[]{:S(2)}) collective-permute-start(f32[512,256]{1,0:T(8,128)} %get-tuple-element.49), channel_id=1, source_target_pairs={{0,1},{1,0},{2,3},{3,2},{4,5},{5,4},{6,7},{7,6},{8,9},{9,8},{10,11... | collective-permute-start | bytes 1572872 | tf_op jit(solution)/shard_map/ppermute | solution.py:322
  42.6 16.4 %collective-permute-start.4 = (f32[512,256]{1,0:T(8,128)}, f32[512,256]{1,0:T(8,128)S(1)}, u32[]{:S(2)}, u32[]{:S(2)}) collective-permute-start(f32[512,256]{1,0:T(8,128)} %get-tuple-element.37), channel_id=1, source_target_pairs={{0,1},{1,0},{2,3},{3,2},{4,5},{5,4},{6,7},{7,6},{8,9},{9,8},{10,11... | collective-permute-start | bytes 1572872 | tf_op jit(solution)/shard_map/ppermute | solution.py:322
  43.1 3.2 %collective-permute-start.2 = (f32[1,196,128]{2,1,0:T(8,128)}, f32[1,196,128]{2,1,0:T(8,128)S(1)}, u32[]{:S(2)}, u32[]{:S(2)}) collective-permute-start(f32[1,196,128]{2,1,0:T(8,128)} %get-tuple-element.34), channel_id=1, source_target_pairs={{0,1},{1,2},{2,3},{3,4},{4,5},{5,6},{6,7},{7,8},{8,9},{9,10},{10,1... | collective-permute-start | bytes 301064 | tf_op jit(solution)/shard_map/ppermute | solution.py:23
  45.1 5.4 %collective-permute-start.3 = (f32[1,196,128]{2,1,0:T(8,128)}, f32[1,196,128]{2,1,0:T(8,128)S(1)}, u32[]{:S(2)}, u32[]{:S(2)}) collective-permute-start(f32[1,196,128]{2,1,0:T(8,128)} %get-tuple-element.35), channel_id=1, source_target_pairs={{1,0},{2,1},{3,2},{4,3},{5,4},{6,5},{7,6},{8,7},{9,8},{10,9},{11,1... | collective-permute-start | bytes 301064 | tf_op jit(solution)/shard_map/ppermute | solution.py:23
  55.8 14.4 %copy-start.7 = (f32[128,256]{1,0:T(8,128)S(1)}, f32[128,256]{1,0:T(8,128)}, u32[]{:S(2)}) copy-start(f32[128,256]{1,0:T(8,128)} %get-tuple-element.39) | copy-start | bytes 393220
  55.8 8.8 %collective-permute-start.13 = (f32[256,256]{1,0:T(8,128)S(1)}, f32[256,256]{1,0:T(8,128)S(1)}, u32[]{:S(2)}, u32[]{:S(2)}) collective-permute-start(f32[256,256]{1,0:T(8,128)S(1)} %slice_add_fusion.3), channel_id=1, source_target_pairs={{0,2},{1,3},{2,0},{3,1},{4,6},{5,7},{6,4},{7,5},{8,10},{9,11},{10,... | collective-permute-start | bytes 786440 | tf_op jit(solution)/shard_map/ppermute | solution.py:322
  59.1 15.2 %copy-start.11 = (f32[64,256]{1,0:T(8,128)S(1)}, f32[64,256]{1,0:T(8,128)}, u32[]{:S(2)}) copy-start(f32[64,256]{1,0:T(8,128)} %get-tuple-element.52) | copy-start | bytes 196612
  59.1 23.7 %copy-start.1 = (f32[288,256]{1,0:T(8,128)S(1)}, f32[288,256]{1,0:T(8,128)}, u32[]{:S(2)}) copy-start(f32[288,256]{1,0:T(8,128)} %get-tuple-element.45) | copy-start | bytes 884740
  59.1 11.1 %collective-permute-start.5 = (f32[256,256]{1,0:T(8,128)S(1)}, f32[256,256]{1,0:T(8,128)S(1)}, u32[]{:S(2)}, u32[]{:S(2)}) collective-permute-start(f32[256,256]{1,0:T(8,128)S(1)} %slice_add_fusion.4), channel_id=1, source_target_pairs={{0,2},{1,3},{2,0},{3,1},{4,6},{5,7},{6,4},{7,5},{8,10},{9,11},{10,... | collective-permute-start | bytes 786440 | tf_op jit(solution)/shard_map/ppermute | solution.py:322
  59.3 27.6 %copy-start.10 = (f32[64,256]{1,0:T(8,128)S(1)}, f32[64,256]{1,0:T(8,128)}, u32[]{:S(2)}) copy-start(f32[64,256]{1,0:T(8,128)} %get-tuple-element.40) | copy-start | bytes 196612
  59.3 29.4 %copy-start.13 = (f32[64,256]{1,0:T(8,128)S(1)}, f32[64,256]{1,0:T(8,128)}, u32[]{:S(2)}) copy-start(f32[64,256]{1,0:T(8,128)} %get-tuple-element.48) | copy-start | bytes 196612
  59.3 23.5 %collective-permute-start.9 = (f32[576,256]{1,0:T(8,128)S(1)}, f32[576,256]{1,0:T(8,128)S(1)}, u32[]{:S(2)}, u32[]{:S(2)}) collective-permute-start(f32[576,256]{1,0:T(8,128)S(1)} %slice_add_fusion), channel_id=1, source_target_pairs={{0,2},{1,3},{2,0},{3,1},{4,6},{5,7},{6,4},{7,5},{8,10},{9,11},{10,... | collective-permute-start | bytes 1769480 | tf_op jit(solution)/shard_map/ppermute | solution.py:322
  64.6 31.2 %copy-start.5 = (f32[144,256]{1,0:T(8,128)S(1)}, f32[144,256]{1,0:T(8,128)}, u32[]{:S(2)}) copy-start(f32[144,256]{1,0:T(8,128)} %get-tuple-element.46) | copy-start | bytes 442372
  64.6 9.7 %collective-permute-start.14 = (f32[128,256]{1,0:T(8,128)S(1)}, f32[128,256]{1,0:T(8,128)S(1)}, u32[]{:S(2)}, u32[]{:S(2)}) collective-permute-start(f32[128,256]{1,0:T(8,128)S(1)} %slice_add_fusion.11), channel_id=1, source_target_pairs={{0,4},{1,5},{2,6},{3,7},{4,0},{5,1},{6,2},{7,3},{8,12},{9,13},{10,... | collective-permute-start | bytes 393224 | tf_op jit(solution)/shard_map/ppermute | solution.py:322
  70.2 27.7 %copy-start.12 = (f32[64,256]{1,0:T(8,128)S(1)}, f32[64,256]{1,0:T(8,128)}, u32[]{:S(2)}) copy-start(f32[64,256]{1,0:T(8,128)} %get-tuple-element.36) | copy-start | bytes 196612
  70.2 16.7 %collective-permute-start.6 = (f32[128,256]{1,0:T(8,128)S(1)}, f32[128,256]{1,0:T(8,128)S(1)}, u32[]{:S(2)}, u32[]{:S(2)}) collective-permute-start(f32[128,256]{1,0:T(8,128)S(1)} %slice_add_fusion.13), channel_id=1, source_target_pairs={{0,4},{1,5},{2,6},{3,7},{4,0},{5,1},{6,2},{7,3},{8,12},{9,13},{10,... | collective-permute-start | bytes 393224 | tf_op jit(solution)/shard_map/ppermute | solution.py:322
  74.2 30.6 %copy-start.4 = (f32[144,256]{1,0:T(8,128)S(1)}, f32[144,256]{1,0:T(8,128)}, u32[]{:S(2)}) copy-start(f32[144,256]{1,0:T(8,128)} %get-tuple-element.42) | copy-start | bytes 442372
  74.3 14.4 %collective-permute-start.15 = (f32[64,256]{1,0:T(8,128)S(1)}, f32[64,256]{1,0:T(8,128)S(1)}, u32[]{:S(2)}, u32[]{:S(2)}) collective-permute-start(f32[64,256]{1,0:T(8,128)S(1)} %slice_add_fusion.15), channel_id=1, source_target_pairs={{0,8},{1,9},{2,10},{3,11},{4,12},{5,13},{6,14},{7,15},{8,0},{9,1},... | collective-permute-start | bytes 196616 | tf_op jit(solution)/shard_map/ppermute | solution.py:322
  82.9 12.9 %collective-permute-start.10 = (f32[288,256]{1,0:T(8,128)S(1)}, f32[288,256]{1,0:T(8,128)S(1)}, u32[]{:S(2)}, u32[]{:S(2)}) collective-permute-start(f32[288,256]{1,0:T(8,128)S(1)} %slice_add_fusion.1), channel_id=1, source_target_pairs={{0,4},{1,5},{2,6},{3,7},{4,0},{5,1},{6,2},{7,3},{8,12},{9,13},{10,... | collective-permute-start | bytes 884744 | tf_op jit(solution)/shard_map/ppermute | solution.py:322
  86.9 11.0 %collective-permute-start.7 = (f32[64,256]{1,0:T(8,128)S(1)}, f32[64,256]{1,0:T(8,128)S(1)}, u32[]{:S(2)}, u32[]{:S(2)}) collective-permute-start(f32[64,256]{1,0:T(8,128)S(1)} %slice_add_fusion.21), channel_id=1, source_target_pairs={{0,8},{1,9},{2,10},{3,11},{4,12},{5,13},{6,14},{7,15},{8,0},{9,1},... | collective-permute-start | bytes 196616 | tf_op jit(solution)/shard_map/ppermute | solution.py:322
  95.8 9.0 %collective-permute-start.11 = (f32[144,256]{1,0:T(8,128)S(1)}, f32[144,256]{1,0:T(8,128)S(1)}, u32[]{:S(2)}, u32[]{:S(2)}) collective-permute-start(f32[144,256]{1,0:T(8,128)S(1)} %slice_add_fusion.5), channel_id=1, source_target_pairs={{0,8},{1,9},{2,10},{3,11},{4,12},{5,13},{6,14},{7,15},{8,0},{9,1},... | collective-permute-start | bytes 442376 | tf_op jit(solution)/shard_map/ppermute | solution.py:322
  (8 other events, 30.9 us)
where the time goes:
time: 106 us
  Pallas kernels  37.7 us (36%)
  starting transfers between devices  35 us (33%)
  waiting for transfers between devices  27 us (25%)
  local copies, waits for them, and re-layouts  2.6 us (2%)
  other arithmetic  2.36 us (2%)
    pallas_call x6, Pallas kernels, call(): pl.pallas_call(kernel, out_shape=list(outs), in_specs=specs, out_specs=[V...  37.7 us
    ppermute x12, starting transfers between devices, scatter_sum(): arrived.append(lax.ppermute(piece, 'tm', route))  27.5 us
    ppermute x12, waiting for transfers between devices, scatter_sum(): arrived.append(lax.ppermute(piece, 'tm', route))  22.9 us
    ppermute x4, starting transfers between devices, passed_along(): return lax.ppermute(block, axis, route)  7.53 us
    ppermute x4, waiting for transfers between devices, passed_along(): return lax.ppermute(block, axis, route)  4.06 us
  transfers between devices with their start and end apart: 16, of which 6 were waited for; matrix products, arithmetic and copies ran while one was open for 2% of the time, Pallas kernels for 20%

commit v1 on v0

--- a/solution.py
+++ b/solution.py
@@ -350,6 +350,9 @@
             return None
         return [1 << b for b in range(shards.bit_length() - 1)]
 
+    def late_second(order):
+        return order if order is None else order[:1] + order[2:] + order[1:2]
+
     def grads(total):
         if order_of(total) is None:
             return [jax.ShapeDtypeStruct((total, middle), F32)]
@@ -393,6 +396,7 @@
         flops=work * (9 * middle + 2 * channels),
     )
     spatial_order, channel_order = order_of(9 * middle), order_of(channels)
+    expand_order = late_second(channel_order)
     spatial_pieces = call(
         functools.partial(spatial_kernel, sz, spatial_order),
         grads(9 * middle),
@@ -403,14 +407,14 @@
     )
     grad_spatial = scatter_sum(sz, spatial_pieces, spatial_order)
     expand_pieces = call(
-        functools.partial(expand_kernel, sz, channel_order),
+        functools.partial(expand_kernel, sz, expand_order),
         grads(channels),
         [me, residual, flat, es],
         [pltpu.VMEM((channels, middle), F32)],
         scalar=True,
         flops=work * channels,
     )
-    grad_expand = scatter_sum(sz, expand_pieces, channel_order)
+    grad_expand = scatter_sum(sz, expand_pieces, expand_order)
     reduce_grad, ahead, behind, *reduce_pieces = call(
         functools.partial(reduce_kernel, sz, channel_order),
         [full(nframes, ncells, middle), full(1, ncells, f), full(1, ncells, f)] + grads(channels),

time: 106 us -> 103 us (0.972)
  starting transfers between devices: 35 us -> 24.5 us
  waiting for transfers between devices: 27 us -> 34.4 us
    ppermute x12, starting transfers between devices: 27.5 us -> 17 us  [scatter_sum(): arrived.append(lax.ppermute(piece, 'tm', route))]
    ppermute x12, waiting for transfers between devices: 22.9 us -> 30.3 us  [scatter_sum(): arrived.append(lax.ppermute(piece, 'tm', route))]
where the time goes in v1:
time: 103 us; the launch traced here: 102 us
  Pallas kernels  37.7 us (37%)
  waiting for transfers between devices  34.4 us (33%)
  starting transfers between devices  24.5 us (24%)
  local copies, waits for them, and re-layouts  2.6 us (3%)
  other arithmetic  2.36 us (2%)
    pallas_call x6, Pallas kernels, call(): pl.pallas_call(kernel, out_shape=list(outs), in_specs=specs, out_specs=[V...  37.7 us
    ppermute x12, waiting for transfers between devices, scatter_sum(): arrived.append(lax.ppermute(piece, 'tm', route))  30.3 us
    ppermute x12, starting transfers between devices, scatter_sum(): arrived.append(lax.ppermute(piece, 'tm', route))  17 us
    ppermute x4, starting transfers between devices, passed_along(): return lax.ppermute(block, axis, route)  7.53 us
    ppermute x4, waiting for transfers between devices, passed_along(): return lax.ppermute(block, axis, route)  4.06 us
  transfers between devices with their start and end apart: 16, of which 6 were waited for; matrix products, arithmetic and copies ran while one was open for 2% of the time, Pallas kernels for 20%

profile of v1, /device:TPU:0, one launch (start us, length us, event | category | flops | bytes accessed | tf_op | source)
XLA Modules:
  0.0 102.4 jit_solution(1239584615335480398)
XLA Ops:
  0.6 1.2 %fusion.3 = (f32[1,196,128]{2,0,1:T(1,128)S(1)}, f32[1,196,128]{2,0,1:T(1,128)S(1)}) fusion(f32[2,196,1024]{2,0,1:T(2,128)} %param.11), kind=kLoop, calls=%fused_computation.30 | loop fusion | bytes 401408 | tf_op jit(solution)/shard_map/slice | solution.py:367
  1.9 1.3 %collective-permute-start = (f32[1,196,128]{2,1,0:T(8,128)S(1)}, f32[1,196,128]{2,1,0:T(8,128)S(1)}, u32[]{:S(2)}, u32[]{:S(2)}) collective-permute-start(f32[1,196,128]{2,1,0:T(8,128)S(1)} %copy.20), channel_id=1, source_target_pairs={{1,0},{2,1},{3,2},{4,3},{5,4},{6,5},{7,6},{8,7},{9,8},{10,9},{11,1... | collective-permute-start | bytes 301064 | tf_op jit(solution)/shard_map/ppermute | solution.py:23
  3.2 3.0 %collective-permute-start.1 = (f32[1,196,128]{2,1,0:T(8,128)S(1)}, f32[1,196,128]{2,1,0:T(8,128)S(1)}, u32[]{:S(2)}, u32[]{:S(2)}) collective-permute-start(f32[1,196,128]{2,1,0:T(8,128)S(1)} %copy.21), channel_id=1, source_target_pairs={{0,1},{1,2},{2,3},{3,4},{4,5},{5,6},{6,7},{7,8},{8,9},{9,10},{10,1... | collective-permute-start | bytes 301064 | tf_op jit(solution)/shard_map/ppermute | solution.py:23
  6.2 3.5 %shard_map.146.part = f32[2,196,256]{2,1,0:T(8,128)} custom-call(f32[3136,128]{1,0:T(8,128)} %bitcast.35, f32[1024,256]{1,0:T(8,128)} %w1.5), custom_call_target="tpu_custom_call" | custom-call | flops 616562688 | bytes 3055616 | tf_op jit(solution)/shard_map/pallas_call | solution.py:301
  10.4 12.4 %shard_map.147 = (f32[3136,128]{1,0:T(8,128)}, f32[2,196,1024]{2,1,0:T(8,128)}, f32[2,272,256]{2,1,0:T(8,128)}, f32[2,272,256]{2,1,0:T(8,128)}, f32[2,196,256]{2,1,0:T(8,128)}, /*index=5*/f32[2,196,256]{2,1,0:T(8,128)}) custom-call(f32[2,196,256]{2,1,0:T(8,128)} %shard_map.146.part, f32[1,196,128]{2,1,0:T(8,128)} %copy-done.14, f32[1,196,128]{2,1,0:T(8,128)} %copy-done.15, ...), custom_call_target="tpu_custom_call" | custom-call | flops 2620391424 | bytes 13410304 | tf_op jit(solution)/shard_map/pallas_call | solution.py:301
  22.8 4.8 %shard_map.150 = (f32[1152,256]{1,0:T(8,128)}, f32[576,256]{1,0:T(8,128)}, f32[288,256]{1,0:T(8,128)}, f32[144,256]{1,0:T(8,128)}, f32[144,256]{1,0:T(8,128)}) custom-call(s32[1]{0:T(128)} %bitcast.18.me_ref, f32[2,272,256]{2,1,0:T(8,128)} %get-tuple-element.41.padded_one, f32[2,272,256]{2,1,0:T(8,128)} %get-tuple-element.30.padded_grad), custom_call_target="tpu_custom_call" | custom-call | flops 1387266048 | bytes 3473412 | tf_op jit(solution)/shard_map/pallas_call | solution.py:301
  27.5 2.6 %collective-permute-start.8 = (f32[1152,256]{1,0:T(8,128)}, f32[1152,256]{1,0:T(8,128)S(1)}, u32[]{:S(2)}, u32[]{:S(2)}) collective-permute-start(f32[1152,256]{1,0:T(8,128)} %get-tuple-element.43), channel_id=1, source_target_pairs={{0,1},{1,0},{2,3},{3,2},{4,5},{5,4},{6,7},{7,6},{8,9},{9,8},{10,11... | collective-permute-start | bytes 3538952 | tf_op jit(solution)/shard_map/ppermute | solution.py:322
  30.2 3.7 %shard_map.151 = (f32[512,256]{1,0:T(8,128)}, f32[256,256]{1,0:T(8,128)}, f32[128,256]{1,0:T(8,128)}, f32[64,256]{1,0:T(8,128)}, f32[64,256]{1,0:T(8,128)}) custom-call(s32[1]{0:T(128)} %bitcast.18.me_ref, f32[2,196,1024]{2,1,0:T(8,128)} %get-tuple-element.33.residual, f32[2,196,256]{2,1,0:T(8,128)} %get-tuple-element.47.flat, f32[1,1024]{1,0:T(1,128)} %bitcast.42), custom_call_target="tpu_custom_call" | custom-call | flops 616562688 | bytes 3059716 | tf_op jit(solution)/shard_map/pallas_call | solution.py:301
  33.9 8.8 %shard_map.148 = (f32[2,196,256]{2,1,0:T(8,128)}, f32[1,196,128]{2,1,0:T(8,128)}, f32[1,196,128]{2,1,0:T(8,128)}, f32[512,256]{1,0:T(8,128)}, f32[256,256]{1,0:T...) custom-call(s32[1]{0:T(128)} %bitcast.18.me_ref, ...), custom_call_target="tpu_custom_call" | custom-call | flops 2003828736 | bytes 7823364 | tf_op jit(solution)/shard_map/pallas_call | solution.py:301
  43.1 1.9 %collective-permute-start.2 = (f32[1,196,128]{2,1,0:T(8,128)}, f32[1,196,128]{2,1,0:T(8,128)S(1)}, u32[]{:S(2)}, u32[]{:S(2)}) collective-permute-start(f32[1,196,128]{2,1,0:T(8,128)} %get-tuple-element.34), channel_id=1, source_target_pairs={{0,1},{1,2},{2,3},{3,4},{4,5},{5,6},{6,7},{7,8},{8,9},{9,10},{10,1... | collective-permute-start | bytes 301064 | tf_op jit(solution)/shard_map/ppermute | solution.py:23
  45.1 1.3 %collective-permute-start.3 = (f32[1,196,128]{2,1,0:T(8,128)}, f32[1,196,128]{2,1,0:T(8,128)S(1)}, u32[]{:S(2)}, u32[]{:S(2)}) collective-permute-start(f32[1,196,128]{2,1,0:T(8,128)} %get-tuple-element.35), channel_id=1, source_target_pairs={{1,0},{2,1},{3,2},{4,3},{5,4},{6,5},{7,6},{8,7},{9,8},{10,9},{11,1... | collective-permute-start | bytes 301064 | tf_op jit(solution)/shard_map/ppermute | solution.py:23
  46.4 4.0 %collective-permute-done.3.after = f32[1,196,128]{2,1,0:T(8,128)S(1)} collective-permute-done((f32[1,196,128]{2,1,0:T(8,128)}, f32[1,196,128]{2,1,0:T(8,128)S(1)}, u32[]{:S(2)}, u32[]{:S(2)}) %collective-permute-start.3) | collective-permute-done | bytes 100384 | tf_op jit(solution)/shard_map/ppermute | solution.py:23
  51.1 4.6 %shard_map.149 = f32[3136,128]{1,0:T(8,128)} custom-call(f32[2,196,256]{2,1,0:T(8,128)} %get-tuple-element.32.reduce_grad, f32[1024,256]{1,0:T(8,128)} %w1.5, f32[2,196,1024]{2,1,0:T(8,128)} %get-tuple-element.33.residual, f32[1,196,128]{2,1,0:T(8,128)} %copy-done.8, f32[1,196,128]{2,1,0:T(8,128)} %copy-done.9), custom_call_target="tpu_custom_call" | custom-call | flops 616562688 | bytes 4861952 | tf_op jit(solution)/shard_map/pallas_call | solution.py:301
  55.8 4.0 %collective-permute-start.13 = (f32[256,256]{1,0:T(8,128)S(1)}, f32[256,256]{1,0:T(8,128)S(1)}, u32[]{:S(2)}, u32[]{:S(2)}) collective-permute-start(f32[256,256]{1,0:T(8,128)S(1)} %slice_add_fusion.3), channel_id=1, source_target_pairs={{0,4},{1,5},{2,6},{3,7},{4,0},{5,1},{6,2},{7,3},{8,12},{9,13},{10,... | collective-permute-start | bytes 786440 | tf_op jit(solution)/shard_map/ppermute | solution.py:322
  59.8 0.9 collective-permute-start.5
  60.8 1.3 %collective-permute-start.9 = (f32[576,256]{1,0:T(8,128)S(1)}, f32[576,256]{1,0:T(8,128)S(1)}, u32[]{:S(2)}, u32[]{:S(2)}) collective-permute-start(f32[576,256]{1,0:T(8,128)S(1)} %slice_add_fusion), channel_id=1, source_target_pairs={{0,2},{1,3},{2,0},{3,1},{4,6},{5,7},{6,4},{7,5},{8,10},{9,11},{10,... | collective-permute-start | bytes 1769480 | tf_op jit(solution)/shard_map/ppermute | solution.py:322
  62.1 4.4 %collective-permute-done.13 = f32[256,256]{1,0:T(8,128)S(1)} collective-permute-done((f32[256,256]{1,0:T(8,128)S(1)}, f32[256,256]{1,0:T(8,128)S(1)}, u32[]{:S(2)}, u32[]{:S(2)}) %collective-permute-start.13) | collective-permute-done | bytes 262176 | tf_op jit(solution)/shard_map/ppermute | solution.py:322
  66.6 3.5 %collective-permute-start.14 = (f32[128,256]{1,0:T(8,128)S(1)}, f32[128,256]{1,0:T(8,128)S(1)}, u32[]{:S(2)}, u32[]{:S(2)}) collective-permute-start(f32[128,256]{1,0:T(8,128)S(1)} %slice_add_fusion.11), channel_id=1, source_target_pairs={{0,8},{1,9},{2,10},{3,11},{4,12},{5,13},{6,14},{7,15},{8,0},{9,1},... | collective-permute-start | bytes 393224 | tf_op jit(solution)/shard_map/ppermute | solution.py:322
  70.4 6.2 %collective-permute-done.14 = f32[128,256]{1,0:T(8,128)S(1)} collective-permute-done((f32[128,256]{1,0:T(8,128)S(1)}, f32[128,256]{1,0:T(8,128)S(1)}, u32[]{:S(2)}, u32[]{:S(2)}) %collective-permute-start.14) | collective-permute-done | bytes 131104 | tf_op jit(solution)/shard_map/ppermute | solution.py:322
  76.8 4.8 %collective-permute-done.9 = f32[576,256]{1,0:T(8,128)S(1)} collective-permute-done((f32[576,256]{1,0:T(8,128)S(1)}, f32[576,256]{1,0:T(8,128)S(1)}, u32[]{:S(2)}, u32[]{:S(2)}) %collective-permute-start.9) | collective-permute-done | bytes 589856 | tf_op jit(solution)/shard_map/ppermute | solution.py:322
  81.8 3.1 %collective-permute-start.7 = (f32[64,256]{1,0:T(8,128)S(1)}, f32[64,256]{1,0:T(8,128)S(1)}, u32[]{:S(2)}, u32[]{:S(2)}) collective-permute-start(f32[64,256]{1,0:T(8,128)S(1)} %slice_add_fusion.21), channel_id=1, source_target_pairs={{0,8},{1,9},{2,10},{3,11},{4,12},{5,13},{6,14},{7,15},{8,0},{9,1},... | collective-permute-start | bytes 196616 | tf_op jit(solution)/shard_map/ppermute | solution.py:322
  85.5 6.9 %collective-permute-done.10 = f32[288,256]{1,0:T(8,128)S(1)} collective-permute-done((f32[288,256]{1,0:T(8,128)S(1)}, f32[288,256]{1,0:T(8,128)S(1)}, u32[]{:S(2)}, u32[]{:S(2)}) %collective-permute-start.10) | collective-permute-done | bytes 294944 | tf_op jit(solution)/shard_map/ppermute | solution.py:322
  93.8 7.9 %collective-permute-done.11 = f32[144,256]{1,0:T(8,128)S(1)} collective-permute-done((f32[144,256]{1,0:T(8,128)S(1)}, f32[144,256]{1,0:T(8,128)S(1)}, u32[]{:S(2)}, u32[]{:S(2)}) %collective-permute-start.11) | collective-permute-done | bytes 147488 | tf_op jit(solution)/shard_map/ppermute | solution.py:322
  101.7 0.7 fusion
  (61 shorter events, 4.7 us)
Async XLA Ops:
  1.9 7.9 %collective-permute-start = (f32[1,196,128]{2,1,0:T(8,128)S(1)}, f32[1,196,128]{2,1,0:T(8,128)S(1)}, u32[]{:S(2)}, u32[]{:S(2)}) collective-permute-start(f32[1,196,128]{2,1,0:T(8,128)S(1)} %copy.20), channel_id=1, source_target_pairs={{1,0},{2,1},{3,2},{4,3},{5,4},{6,5},{7,6},{8,7},{9,8},{10,9},{11,1... | collective-permute-start | bytes 301064 | tf_op jit(solution)/shard_map/ppermute | solution.py:23
  3.2 6.6 %collective-permute-start.1 = (f32[1,196,128]{2,1,0:T(8,128)S(1)}, f32[1,196,128]{2,1,0:T(8,128)S(1)}, u32[]{:S(2)}, u32[]{:S(2)}) collective-permute-start(f32[1,196,128]{2,1,0:T(8,128)S(1)} %copy.21), channel_id=1, source_target_pairs={{0,1},{1,2},{2,3},{3,4},{4,5},{5,6},{6,7},{7,8},{8,9},{9,10},{10,1... | collective-permute-start | bytes 301064 | tf_op jit(solution)/shard_map/ppermute | solution.py:23
  27.5 33.2 %collective-permute-start.8 = (f32[1152,256]{1,0:T(8,128)}, f32[1152,256]{1,0:T(8,128)S(1)}, u32[]{:S(2)}, u32[]{:S(2)}) collective-permute-start(f32[1152,256]{1,0:T(8,128)} %get-tuple-element.43), channel_id=1, source_target_pairs={{0,1},{1,0},{2,3},{3,2},{4,5},{5,4},{6,7},{7,6},{8,9},{9,8},{10,11... | collective-permute-start | bytes 3538952 | tf_op jit(solution)/shard_map/ppermute | solution.py:322
  33.9 21.8 %collective-permute-start.12 = (f32[512,256]{1,0:T(8,128)}, f32[512,256]{1,0:T(8,128)S(1)}, u32[]{:S(2)}, u32[]{:S(2)}) collective-permute-start(f32[512,256]{1,0:T(8,128)} %get-tuple-element.49), channel_id=1, source_target_pairs={{0,1},{1,0},{2,3},{3,2},{4,5},{5,4},{6,7},{7,6},{8,9},{9,8},{10,11... | collective-permute-start | bytes 1572872 | tf_op jit(solution)/shard_map/ppermute | solution.py:322
  42.6 17.1 %collective-permute-start.4 = (f32[512,256]{1,0:T(8,128)}, f32[512,256]{1,0:T(8,128)S(1)}, u32[]{:S(2)}, u32[]{:S(2)}) collective-permute-start(f32[512,256]{1,0:T(8,128)} %get-tuple-element.37), channel_id=1, source_target_pairs={{0,1},{1,0},{2,3},{3,2},{4,5},{5,4},{6,7},{7,6},{8,9},{9,8},{10,11... | collective-permute-start | bytes 1572872 | tf_op jit(solution)/shard_map/ppermute | solution.py:322
  43.1 3.2 %collective-permute-start.2 = (f32[1,196,128]{2,1,0:T(8,128)}, f32[1,196,128]{2,1,0:T(8,128)S(1)}, u32[]{:S(2)}, u32[]{:S(2)}) collective-permute-start(f32[1,196,128]{2,1,0:T(8,128)} %get-tuple-element.34), channel_id=1, source_target_pairs={{0,1},{1,2},{2,3},{3,4},{4,5},{5,6},{6,7},{7,8},{8,9},{9,10},{10,1... | collective-permute-start | bytes 301064 | tf_op jit(solution)/shard_map/ppermute | solution.py:23
  45.1 5.4 %collective-permute-start.3 = (f32[1,196,128]{2,1,0:T(8,128)}, f32[1,196,128]{2,1,0:T(8,128)S(1)}, u32[]{:S(2)}, u32[]{:S(2)}) collective-permute-start(f32[1,196,128]{2,1,0:T(8,128)} %get-tuple-element.35), channel_id=1, source_target_pairs={{1,0},{2,1},{3,2},{4,3},{5,4},{6,5},{7,6},{8,7},{9,8},{10,9},{11,1... | collective-permute-start | bytes 301064 | tf_op jit(solution)/shard_map/ppermute | solution.py:23
  55.8 14.3 %copy-start.7 = (f32[128,256]{1,0:T(8,128)S(1)}, f32[128,256]{1,0:T(8,128)}, u32[]{:S(2)}) copy-start(f32[128,256]{1,0:T(8,128)} %get-tuple-element.39) | copy-start | bytes 393220
  55.8 10.7 %collective-permute-start.13 = (f32[256,256]{1,0:T(8,128)S(1)}, f32[256,256]{1,0:T(8,128)S(1)}, u32[]{:S(2)}, u32[]{:S(2)}) collective-permute-start(f32[256,256]{1,0:T(8,128)S(1)} %slice_add_fusion.3), channel_id=1, source_target_pairs={{0,4},{1,5},{2,6},{3,7},{4,0},{5,1},{6,2},{7,3},{8,12},{9,13},{10,... | collective-permute-start | bytes 786440 | tf_op jit(solution)/shard_map/ppermute | solution.py:322
  59.8 16.9 %copy-start.11 = (f32[64,256]{1,0:T(8,128)S(1)}, f32[64,256]{1,0:T(8,128)}, u32[]{:S(2)}) copy-start(f32[64,256]{1,0:T(8,128)} %get-tuple-element.52) | copy-start | bytes 196612
  59.8 21.8 %copy-start.1 = (f32[288,256]{1,0:T(8,128)S(1)}, f32[288,256]{1,0:T(8,128)}, u32[]{:S(2)}) copy-start(f32[288,256]{1,0:T(8,128)} %get-tuple-element.45) | copy-start | bytes 884740
  59.8 10.2 %collective-permute-start.5 = (f32[256,256]{1,0:T(8,128)S(1)}, f32[256,256]{1,0:T(8,128)S(1)}, u32[]{:S(2)}, u32[]{:S(2)}) collective-permute-start(f32[256,256]{1,0:T(8,128)S(1)} %slice_add_fusion.4), channel_id=1, source_target_pairs={{0,2},{1,3},{2,0},{3,1},{4,6},{5,7},{6,4},{7,5},{8,10},{9,11},{10,... | collective-permute-start | bytes 786440 | tf_op jit(solution)/shard_map/ppermute | solution.py:322
  60.8 20.9 %copy-start.10 = (f32[64,256]{1,0:T(8,128)S(1)}, f32[64,256]{1,0:T(8,128)}, u32[]{:S(2)}) copy-start(f32[64,256]{1,0:T(8,128)} %get-tuple-element.40) | copy-start | bytes 196612
  60.8 24.0 %copy-start.13 = (f32[64,256]{1,0:T(8,128)S(1)}, f32[64,256]{1,0:T(8,128)}, u32[]{:S(2)}) copy-start(f32[64,256]{1,0:T(8,128)} %get-tuple-element.48) | copy-start | bytes 196612
  60.8 20.7 %collective-permute-start.9 = (f32[576,256]{1,0:T(8,128)S(1)}, f32[576,256]{1,0:T(8,128)S(1)}, u32[]{:S(2)}, u32[]{:S(2)}) collective-permute-start(f32[576,256]{1,0:T(8,128)S(1)} %slice_add_fusion), channel_id=1, source_target_pairs={{0,2},{1,3},{2,0},{3,1},{4,6},{5,7},{6,4},{7,5},{8,10},{9,11},{10,... | collective-permute-start | bytes 1769480 | tf_op jit(solution)/shard_map/ppermute | solution.py:322
  66.5 25.9 %copy-start.5 = (f32[144,256]{1,0:T(8,128)S(1)}, f32[144,256]{1,0:T(8,128)}, u32[]{:S(2)}) copy-start(f32[144,256]{1,0:T(8,128)} %get-tuple-element.46) | copy-start | bytes 442372
  66.6 10.1 %collective-permute-start.14 = (f32[128,256]{1,0:T(8,128)S(1)}, f32[128,256]{1,0:T(8,128)S(1)}, u32[]{:S(2)}, u32[]{:S(2)}) collective-permute-start(f32[128,256]{1,0:T(8,128)S(1)} %slice_add_fusion.11), channel_id=1, source_target_pairs={{0,8},{1,9},{2,10},{3,11},{4,12},{5,13},{6,14},{7,15},{8,0},{9,1},... | collective-permute-start | bytes 393224 | tf_op jit(solution)/shard_map/ppermute | solution.py:322
  70.1 23.1 %copy-start.12 = (f32[64,256]{1,0:T(8,128)S(1)}, f32[64,256]{1,0:T(8,128)}, u32[]{:S(2)}) copy-start(f32[64,256]{1,0:T(8,128)} %get-tuple-element.36) | copy-start | bytes 196612
  70.1 11.7 %collective-permute-start.6 = (f32[128,256]{1,0:T(8,128)S(1)}, f32[128,256]{1,0:T(8,128)S(1)}, u32[]{:S(2)}, u32[]{:S(2)}) collective-permute-start(f32[128,256]{1,0:T(8,128)S(1)} %slice_add_fusion.13), channel_id=1, source_target_pairs={{0,4},{1,5},{2,6},{3,7},{4,0},{5,1},{6,2},{7,3},{8,12},{9,13},{10,... | collective-permute-start | bytes 393224 | tf_op jit(solution)/shard_map/ppermute | solution.py:322
  76.7 25.1 %copy-start.4 = (f32[144,256]{1,0:T(8,128)S(1)}, f32[144,256]{1,0:T(8,128)}, u32[]{:S(2)}) copy-start(f32[144,256]{1,0:T(8,128)} %get-tuple-element.42) | copy-start | bytes 442372
  76.7 8.2 %collective-permute-start.15 = (f32[64,256]{1,0:T(8,128)S(1)}, f32[64,256]{1,0:T(8,128)S(1)}, u32[]{:S(2)}, u32[]{:S(2)}) collective-permute-start(f32[64,256]{1,0:T(8,128)S(1)} %slice_add_fusion.15), channel_id=1, source_target_pairs={{0,2},{1,3},{2,0},{3,1},{4,6},{5,7},{6,4},{7,5},{8,10},{9,11},{10,... | collective-permute-start | bytes 196616 | tf_op jit(solution)/shard_map/ppermute | solution.py:322
  81.6 10.8 %collective-permute-start.10 = (f32[288,256]{1,0:T(8,128)S(1)}, f32[288,256]{1,0:T(8,128)S(1)}, u32[]{:S(2)}, u32[]{:S(2)}) collective-permute-start(f32[288,256]{1,0:T(8,128)S(1)} %slice_add_fusion.1), channel_id=1, source_target_pairs={{0,4},{1,5},{2,6},{3,7},{4,0},{5,1},{6,2},{7,3},{8,12},{9,13},{10,... | collective-permute-start | bytes 884744 | tf_op jit(solution)/shard_map/ppermute | solution.py:322
  81.8 11.4 %collective-permute-start.7 = (f32[64,256]{1,0:T(8,128)S(1)}, f32[64,256]{1,0:T(8,128)S(1)}, u32[]{:S(2)}, u32[]{:S(2)}) collective-permute-start(f32[64,256]{1,0:T(8,128)S(1)} %slice_add_fusion.21), channel_id=1, source_target_pairs={{0,8},{1,9},{2,10},{3,11},{4,12},{5,13},{6,14},{7,15},{8,0},{9,1},... | collective-permute-start | bytes 196616 | tf_op jit(solution)/shard_map/ppermute | solution.py:322
  92.5 9.3 %collective-permute-start.11 = (f32[144,256]{1,0:T(8,128)S(1)}, f32[144,256]{1,0:T(8,128)S(1)}, u32[]{:S(2)}, u32[]{:S(2)}) collective-permute-start(f32[144,256]{1,0:T(8,128)S(1)} %slice_add_fusion.5), channel_id=1, source_target_pairs={{0,8},{1,9},{2,10},{3,11},{4,12},{5,13},{6,14},{7,15},{8,0},{9,1},... | collective-permute-start | bytes 442376 | tf_op jit(solution)/shard_map/ppermute | solution.py:322
  (8 other events, 35.2 us)

commit v2 on v1

--- a/solution.py
+++ b/solution.py
@@ -38,12 +38,9 @@
 
 def gelu_pair(values):
     square = values * values
-    turned = jnp.tanh(ROOT * values * (1.0 + CUBE * square))
-    half = 0.5 * (1.0 + turned)
-    slope = half + (0.5 * ROOT) * values * (1.0 - turned * turned) * (
-        1.0 + (3.0 * CUBE) * square
-    )
-    return values * half, slope
+    half = 0.5 * jnp.tanh(values * ((ROOT * CUBE) * square + ROOT)) + 0.5
+    inner = values * ((6.0 * ROOT * CUBE) * square + 2.0 * ROOT)
+    return values * half, half * (1.0 + (1.0 - half) * inner)
 
 
 def pick(pair, index):
@@ -351,7 +348,7 @@
         return [1 << b for b in range(shards.bit_length() - 1)]
 
     def late_second(order):
-        return order if order is None else order[:1] + order[2:] + order[1:2]
+        return order if order is None else order[:1] + order[2:3] + order[1:2] + order[3:]
 
     def grads(total):
         if order_of(total) is None:

time: 103 us -> 106 us (1.029)
  waiting for transfers between devices: 34.4 us -> 42 us
  starting transfers between devices: 24.5 us -> 20.7 us
    ppermute x12, waiting for transfers between devices: 30.3 us -> 37.9 us  [scatter_sum(): arrived.append(lax.ppermute(piece, 'tm', route))]
    ppermute x12, starting transfers between devices: 17 us -> 13.2 us  [scatter_sum(): arrived.append(lax.ppermute(piece, 'tm', route))]
  transfers between devices with their start and end apart: 16 -> 16, of which waited for: 6 -> 7; matrix products, arithmetic and copies ran while one was open for 2% -> 2% of each run, Pallas kernels for 20% -> 19%
where the time goes in v2:
time: 106 us
  waiting for transfers between devices  42 us (40%)
  Pallas kernels  37.6 us (35%)
  starting transfers between devices  20.7 us (20%)
  local copies, waits for them, and re-layouts  2.6 us (2%)
  other arithmetic  2.36 us (2%)
    ppermute x12, waiting for transfers between devices, scatter_sum(): arrived.append(lax.ppermute(piece, 'tm', route))  37.9 us
    pallas_call x6, Pallas kernels, call(): pl.pallas_call(kernel, out_shape=list(outs), in_specs=specs, out_specs=[V...  37.6 us
    ppermute x12, starting transfers between devices, scatter_sum(): arrived.append(lax.ppermute(piece, 'tm', route))  13.2 us
    ppermute x4, starting transfers between devices, passed_along(): return lax.ppermute(block, axis, route)  7.53 us
    ppermute x4, waiting for transfers between devices, passed_along(): return lax.ppermute(block, axis, route)  4.06 us
  transfers between devices with their start and end apart: 16, of which 7 were waited for; matrix products, arithmetic and copies ran while one was open for 2% of the time, Pallas kernels for 19%

profile of v2, /device:TPU:0, one launch (start us, length us, event | category | flops | bytes accessed | tf_op | source)
XLA Modules:
  0.0 106.1 jit_solution(15619756218818409480)
XLA Ops:
  0.6 1.2 %fusion.3 = (f32[1,196,128]{2,0,1:T(1,128)S(1)}, f32[1,196,128]{2,0,1:T(1,128)S(1)}) fusion(f32[2,196,1024]{2,0,1:T(2,128)} %param.11), kind=kLoop, calls=%fused_computation.30 | loop fusion | bytes 401408 | tf_op jit(solution)/shard_map/slice | solution.py:364
  1.9 1.3 %collective-permute-start = (f32[1,196,128]{2,1,0:T(8,128)S(1)}, f32[1,196,128]{2,1,0:T(8,128)S(1)}, u32[]{:S(2)}, u32[]{:S(2)}) collective-permute-start(f32[1,196,128]{2,1,0:T(8,128)S(1)} %copy.20), channel_id=1, source_target_pairs={{1,0},{2,1},{3,2},{4,3},{5,4},{6,5},{7,6},{8,7},{9,8},{10,9},{11,1... | collective-permute-start | bytes 301064 | tf_op jit(solution)/shard_map/ppermute | solution.py:23
  3.2 3.0 %collective-permute-start.1 = (f32[1,196,128]{2,1,0:T(8,128)S(1)}, f32[1,196,128]{2,1,0:T(8,128)S(1)}, u32[]{:S(2)}, u32[]{:S(2)}) collective-permute-start(f32[1,196,128]{2,1,0:T(8,128)S(1)} %copy.21), channel_id=1, source_target_pairs={{0,1},{1,2},{2,3},{3,4},{4,5},{5,6},{6,7},{7,8},{8,9},{9,10},{10,1... | collective-permute-start | bytes 301064 | tf_op jit(solution)/shard_map/ppermute | solution.py:23
  6.2 3.5 %shard_map.146.part = f32[2,196,256]{2,1,0:T(8,128)} custom-call(f32[3136,128]{1,0:T(8,128)} %bitcast.35, f32[1024,256]{1,0:T(8,128)} %w1.5), custom_call_target="tpu_custom_call" | custom-call | flops 616562688 | bytes 3055616 | tf_op jit(solution)/shard_map/pallas_call | solution.py:298
  10.4 12.3 %shard_map.147 = (f32[3136,128]{1,0:T(8,128)}, f32[2,196,1024]{2,1,0:T(8,128)}, f32[2,272,256]{2,1,0:T(8,128)}, f32[2,272,256]{2,1,0:T(8,128)}, f32[2,196,256]{2,1,0:T(8,128)}, /*index=5*/f32[2,196,256]{2,1,0:T(8,128)}) custom-call(f32[2,196,256]{2,1,0:T(8,128)} %shard_map.146.part, f32[1,196,128]{2,1,0:T(8,128)} %copy-done.14, f32[1,196,128]{2,1,0:T(8,128)} %copy-done.15, ...), custom_call_target="tpu_custom_call" | custom-call | flops 2620391424 | bytes 13410304 | tf_op jit(solution)/shard_map/pallas_call | solution.py:298
  22.7 4.8 %shard_map.150 = (f32[1152,256]{1,0:T(8,128)}, f32[576,256]{1,0:T(8,128)}, f32[288,256]{1,0:T(8,128)}, f32[144,256]{1,0:T(8,128)}, f32[144,256]{1,0:T(8,128)}) custom-call(s32[1]{0:T(128)} %bitcast.18.me_ref, f32[2,272,256]{2,1,0:T(8,128)} %get-tuple-element.41.padded_one, f32[2,272,256]{2,1,0:T(8,128)} %get-tuple-element.30.padded_grad), custom_call_target="tpu_custom_call" | custom-call | flops 1387266048 | bytes 3473412 | tf_op jit(solution)/shard_map/pallas_call | solution.py:298
  27.5 2.6 %collective-permute-start.8 = (f32[1152,256]{1,0:T(8,128)}, f32[1152,256]{1,0:T(8,128)S(1)}, u32[]{:S(2)}, u32[]{:S(2)}) collective-permute-start(f32[1152,256]{1,0:T(8,128)} %get-tuple-element.43), channel_id=1, source_target_pairs={{0,1},{1,0},{2,3},{3,2},{4,5},{5,4},{6,7},{7,6},{8,9},{9,8},{10,11... | collective-permute-start | bytes 3538952 | tf_op jit(solution)/shard_map/ppermute | solution.py:319
  30.1 3.7 %shard_map.151 = (f32[512,256]{1,0:T(8,128)}, f32[256,256]{1,0:T(8,128)}, f32[128,256]{1,0:T(8,128)}, f32[64,256]{1,0:T(8,128)}, f32[64,256]{1,0:T(8,128)}) custom-call(s32[1]{0:T(128)} %bitcast.18.me_ref, f32[2,196,1024]{2,1,0:T(8,128)} %get-tuple-element.33.residual, f32[2,196,256]{2,1,0:T(8,128)} %get-tuple-element.47.flat, f32[1,1024]{1,0:T(1,128)} %bitcast.42), custom_call_target="tpu_custom_call" | custom-call | flops 616562688 | bytes 3059716 | tf_op jit(solution)/shard_map/pallas_call | solution.py:298
  33.8 8.8 %shard_map.148 = (f32[2,196,256]{2,1,0:T(8,128)}, f32[1,196,128]{2,1,0:T(8,128)}, f32[1,196,128]{2,1,0:T(8,128)}, f32[512,256]{1,0:T(8,128)}, f32[256,256]{1,0:T...) custom-call(s32[1]{0:T(128)} %bitcast.18.me_ref, ...), custom_call_target="tpu_custom_call" | custom-call | flops 2003828736 | bytes 7823364 | tf_op jit(solution)/shard_map/pallas_call | solution.py:298
  43.1 1.9 %collective-permute-start.2 = (f32[1,196,128]{2,1,0:T(8,128)}, f32[1,196,128]{2,1,0:T(8,128)S(1)}, u32[]{:S(2)}, u32[]{:S(2)}) collective-permute-start(f32[1,196,128]{2,1,0:T(8,128)} %get-tuple-element.34), channel_id=1, source_target_pairs={{0,1},{1,2},{2,3},{3,4},{4,5},{5,6},{6,7},{7,8},{8,9},{9,10},{10,1... | collective-permute-start | bytes 301064 | tf_op jit(solution)/shard_map/ppermute | solution.py:23
  45.0 1.3 %collective-permute-start.3 = (f32[1,196,128]{2,1,0:T(8,128)}, f32[1,196,128]{2,1,0:T(8,128)S(1)}, u32[]{:S(2)}, u32[]{:S(2)}) collective-permute-start(f32[1,196,128]{2,1,0:T(8,128)} %get-tuple-element.35), channel_id=1, source_target_pairs={{1,0},{2,1},{3,2},{4,3},{5,4},{6,5},{7,6},{8,7},{9,8},{10,9},{11,1... | collective-permute-start | bytes 301064 | tf_op jit(solution)/shard_map/ppermute | solution.py:23
  46.3 4.0 %collective-permute-done.3.after = f32[1,196,128]{2,1,0:T(8,128)S(1)} collective-permute-done((f32[1,196,128]{2,1,0:T(8,128)}, f32[1,196,128]{2,1,0:T(8,128)S(1)}, u32[]{:S(2)}, u32[]{:S(2)}) %collective-permute-start.3) | collective-permute-done | bytes 100384 | tf_op jit(solution)/shard_map/ppermute | solution.py:23
  51.0 4.6 %shard_map.149 = f32[3136,128]{1,0:T(8,128)} custom-call(f32[2,196,256]{2,1,0:T(8,128)} %get-tuple-element.32.reduce_grad, f32[1024,256]{1,0:T(8,128)} %w1.5, f32[2,196,1024]{2,1,0:T(8,128)} %get-tuple-element.33.residual, f32[1,196,128]{2,1,0:T(8,128)} %copy-done.8, f32[1,196,128]{2,1,0:T(8,128)} %copy-done.9), custom_call_target="tpu_custom_call" | custom-call | flops 616562688 | bytes 4861952 | tf_op jit(solution)/shard_map/pallas_call | solution.py:298
  55.7 4.0 %collective-permute-start.13 = (f32[256,256]{1,0:T(8,128)S(1)}, f32[256,256]{1,0:T(8,128)S(1)}, u32[]{:S(2)}, u32[]{:S(2)}) collective-permute-start(f32[256,256]{1,0:T(8,128)S(1)} %slice_add_fusion.3), channel_id=1, source_target_pairs={{0,4},{1,5},{2,6},{3,7},{4,0},{5,1},{6,2},{7,3},{8,12},{9,13},{10,... | collective-permute-start | bytes 786440 | tf_op jit(solution)/shard_map/ppermute | solution.py:319
  59.7 0.9 collective-permute-start.5
  60.7 1.3 %collective-permute-start.9 = (f32[576,256]{1,0:T(8,128)S(1)}, f32[576,256]{1,0:T(8,128)S(1)}, u32[]{:S(2)}, u32[]{:S(2)}) collective-permute-start(f32[576,256]{1,0:T(8,128)S(1)} %slice_add_fusion), channel_id=1, source_target_pairs={{0,2},{1,3},{2,0},{3,1},{4,6},{5,7},{6,4},{7,5},{8,10},{9,11},{10,... | collective-permute-start | bytes 1769480 | tf_op jit(solution)/shard_map/ppermute | solution.py:319
  62.0 4.4 %collective-permute-done.13 = f32[256,256]{1,0:T(8,128)S(1)} collective-permute-done((f32[256,256]{1,0:T(8,128)S(1)}, f32[256,256]{1,0:T(8,128)S(1)}, u32[]{:S(2)}, u32[]{:S(2)}) %collective-permute-start.13) | collective-permute-done | bytes 262176 | tf_op jit(solution)/shard_map/ppermute | solution.py:319
  66.9 2.0 %collective-permute-done.5 = f32[256,256]{1,0:T(8,128)S(1)} collective-permute-done((f32[256,256]{1,0:T(8,128)S(1)}, f32[256,256]{1,0:T(8,128)S(1)}, u32[]{:S(2)}, u32[]{:S(2)}) %collective-permute-start.5) | collective-permute-done | bytes 262176 | tf_op jit(solution)/shard_map/ppermute | solution.py:319
  69.1 15.2 %collective-permute-done.14 = f32[128,256]{1,0:T(8,128)S(1)} collective-permute-done((f32[128,256]{1,0:T(8,128)S(1)}, f32[128,256]{1,0:T(8,128)S(1)}, u32[]{:S(2)}, u32[]{:S(2)}) %collective-permute-start.14) | collective-permute-done | bytes 131104 | tf_op jit(solution)/shard_map/ppermute | solution.py:319
  84.3 1.7 %collective-permute-start.15 = (f32[64,256]{1,0:T(8,128)S(1)}, f32[64,256]{1,0:T(8,128)S(1)}, u32[]{:S(2)}, u32[]{:S(2)}) collective-permute-start(f32[64,256]{1,0:T(8,128)S(1)} %slice_add_fusion.15), channel_id=1, source_target_pairs={{0,8},{1,9},{2,10},{3,11},{4,12},{5,13},{6,14},{7,15},{8,0},{9,1},... | collective-permute-start | bytes 196616 | tf_op jit(solution)/shard_map/ppermute | solution.py:319
  86.1 1.5 %collective-permute-start.10 = (f32[288,256]{1,0:T(8,128)S(1)}, f32[288,256]{1,0:T(8,128)S(1)}, u32[]{:S(2)}, u32[]{:S(2)}) collective-permute-start(f32[288,256]{1,0:T(8,128)S(1)} %slice_add_fusion.1), channel_id=1, source_target_pairs={{0,4},{1,5},{2,6},{3,7},{4,0},{5,1},{6,2},{7,3},{8,12},{9,13},{10,... | collective-permute-start | bytes 884744 | tf_op jit(solution)/shard_map/ppermute | solution.py:319
  87.7 3.1 %collective-permute-done.15 = f32[64,256]{1,0:T(8,128)S(1)} collective-permute-done((f32[64,256]{1,0:T(8,128)S(1)}, f32[64,256]{1,0:T(8,128)S(1)}, u32[]{:S(2)}, u32[]{:S(2)}) %collective-permute-start.15) | collective-permute-done | bytes 65568 | tf_op jit(solution)/shard_map/ppermute | solution.py:319
  91.4 6.0 %collective-permute-done.10 = f32[288,256]{1,0:T(8,128)S(1)} collective-permute-done((f32[288,256]{1,0:T(8,128)S(1)}, f32[288,256]{1,0:T(8,128)S(1)}, u32[]{:S(2)}, u32[]{:S(2)}) %collective-permute-start.10) | collective-permute-done | bytes 294944 | tf_op jit(solution)/shard_map/ppermute | solution.py:319
  98.1 7.3 %collective-permute-done.11 = f32[144,256]{1,0:T(8,128)S(1)} collective-permute-done((f32[144,256]{1,0:T(8,128)S(1)}, f32[144,256]{1,0:T(8,128)S(1)}, u32[]{:S(2)}, u32[]{:S(2)}) %collective-permute-start.11) | collective-permute-done | bytes 147488 | tf_op jit(solution)/shard_map/ppermute | solution.py:319
  (61 shorter events, 5.0 us)
Async XLA Ops:
  1.9 7.9 %collective-permute-start = (f32[1,196,128]{2,1,0:T(8,128)S(1)}, f32[1,196,128]{2,1,0:T(8,128)S(1)}, u32[]{:S(2)}, u32[]{:S(2)}) collective-permute-start(f32[1,196,128]{2,1,0:T(8,128)S(1)} %copy.20), channel_id=1, source_target_pairs={{1,0},{2,1},{3,2},{4,3},{5,4},{6,5},{7,6},{8,7},{9,8},{10,9},{11,1... | collective-permute-start | bytes 301064 | tf_op jit(solution)/shard_map/ppermute | solution.py:23
  3.2 6.6 %collective-permute-start.1 = (f32[1,196,128]{2,1,0:T(8,128)S(1)}, f32[1,196,128]{2,1,0:T(8,128)S(1)}, u32[]{:S(2)}, u32[]{:S(2)}) collective-permute-start(f32[1,196,128]{2,1,0:T(8,128)S(1)} %copy.21), channel_id=1, source_target_pairs={{0,1},{1,2},{2,3},{3,4},{4,5},{5,6},{6,7},{7,8},{8,9},{9,10},{10,1... | collective-permute-start | bytes 301064 | tf_op jit(solution)/shard_map/ppermute | solution.py:23
  27.5 33.2 %collective-permute-start.8 = (f32[1152,256]{1,0:T(8,128)}, f32[1152,256]{1,0:T(8,128)S(1)}, u32[]{:S(2)}, u32[]{:S(2)}) collective-permute-start(f32[1152,256]{1,0:T(8,128)} %get-tuple-element.43), channel_id=1, source_target_pairs={{0,1},{1,0},{2,3},{3,2},{4,5},{5,4},{6,7},{7,6},{8,9},{9,8},{10,11... | collective-permute-start | bytes 3538952 | tf_op jit(solution)/shard_map/ppermute | solution.py:319
  33.8 21.8 %collective-permute-start.12 = (f32[512,256]{1,0:T(8,128)}, f32[512,256]{1,0:T(8,128)S(1)}, u32[]{:S(2)}, u32[]{:S(2)}) collective-permute-start(f32[512,256]{1,0:T(8,128)} %get-tuple-element.49), channel_id=1, source_target_pairs={{0,1},{1,0},{2,3},{3,2},{4,5},{5,4},{6,7},{7,6},{8,9},{9,8},{10,11... | collective-permute-start | bytes 1572872 | tf_op jit(solution)/shard_map/ppermute | solution.py:319
  42.6 17.1 %collective-permute-start.4 = (f32[512,256]{1,0:T(8,128)}, f32[512,256]{1,0:T(8,128)S(1)}, u32[]{:S(2)}, u32[]{:S(2)}) collective-permute-start(f32[512,256]{1,0:T(8,128)} %get-tuple-element.37), channel_id=1, source_target_pairs={{0,1},{1,0},{2,3},{3,2},{4,5},{5,4},{6,7},{7,6},{8,9},{9,8},{10,11... | collective-permute-start | bytes 1572872 | tf_op jit(solution)/shard_map/ppermute | solution.py:319
  43.1 3.2 %collective-permute-start.2 = (f32[1,196,128]{2,1,0:T(8,128)}, f32[1,196,128]{2,1,0:T(8,128)S(1)}, u32[]{:S(2)}, u32[]{:S(2)}) collective-permute-start(f32[1,196,128]{2,1,0:T(8,128)} %get-tuple-element.34), channel_id=1, source_target_pairs={{0,1},{1,2},{2,3},{3,4},{4,5},{5,6},{6,7},{7,8},{8,9},{9,10},{10,1... | collective-permute-start | bytes 301064 | tf_op jit(solution)/shard_map/ppermute | solution.py:23
  45.0 5.4 %collective-permute-start.3 = (f32[1,196,128]{2,1,0:T(8,128)}, f32[1,196,128]{2,1,0:T(8,128)S(1)}, u32[]{:S(2)}, u32[]{:S(2)}) collective-permute-start(f32[1,196,128]{2,1,0:T(8,128)} %get-tuple-element.35), channel_id=1, source_target_pairs={{1,0},{2,1},{3,2},{4,3},{5,4},{6,5},{7,6},{8,7},{9,8},{10,9},{11,1... | collective-permute-start | bytes 301064 | tf_op jit(solution)/shard_map/ppermute | solution.py:23
  55.7 13.2 %copy-start.7 = (f32[128,256]{1,0:T(8,128)S(1)}, f32[128,256]{1,0:T(8,128)}, u32[]{:S(2)}) copy-start(f32[128,256]{1,0:T(8,128)} %get-tuple-element.39) | copy-start | bytes 393220
  55.7 10.7 %collective-permute-start.13 = (f32[256,256]{1,0:T(8,128)S(1)}, f32[256,256]{1,0:T(8,128)S(1)}, u32[]{:S(2)}, u32[]{:S(2)}) collective-permute-start(f32[256,256]{1,0:T(8,128)S(1)} %slice_add_fusion.3), channel_id=1, source_target_pairs={{0,4},{1,5},{2,6},{3,7},{4,0},{5,1},{6,2},{7,3},{8,12},{9,13},{10,... | collective-permute-start | bytes 786440 | tf_op jit(solution)/shard_map/ppermute | solution.py:319
  59.7 24.6 %copy-start.11 = (f32[64,256]{1,0:T(8,128)S(1)}, f32[64,256]{1,0:T(8,128)}, u32[]{:S(2)}) copy-start(f32[64,256]{1,0:T(8,128)} %get-tuple-element.52) | copy-start | bytes 196612
  59.7 26.3 %copy-start.1 = (f32[288,256]{1,0:T(8,128)S(1)}, f32[288,256]{1,0:T(8,128)}, u32[]{:S(2)}) copy-start(f32[288,256]{1,0:T(8,128)} %get-tuple-element.45) | copy-start | bytes 884740
  59.7 9.1 %collective-permute-start.5 = (f32[256,256]{1,0:T(8,128)S(1)}, f32[256,256]{1,0:T(8,128)S(1)}, u32[]{:S(2)}, u32[]{:S(2)}) collective-permute-start(f32[256,256]{1,0:T(8,128)S(1)} %slice_add_fusion.4), channel_id=1, source_target_pairs={{0,2},{1,3},{2,0},{3,1},{4,6},{5,7},{6,4},{7,5},{8,10},{9,11},{10,... | collective-permute-start | bytes 786440 | tf_op jit(solution)/shard_map/ppermute | solution.py:319
  60.7 26.8 %copy-start.10 = (f32[64,256]{1,0:T(8,128)S(1)}, f32[64,256]{1,0:T(8,128)}, u32[]{:S(2)}) copy-start(f32[64,256]{1,0:T(8,128)} %get-tuple-element.40) | copy-start | bytes 196612
  60.7 30.0 %copy-start.13 = (f32[64,256]{1,0:T(8,128)S(1)}, f32[64,256]{1,0:T(8,128)}, u32[]{:S(2)}) copy-start(f32[64,256]{1,0:T(8,128)} %get-tuple-element.48) | copy-start | bytes 196612
  60.7 25.3 %collective-permute-start.9 = (f32[576,256]{1,0:T(8,128)S(1)}, f32[576,256]{1,0:T(8,128)S(1)}, u32[]{:S(2)}, u32[]{:S(2)}) collective-permute-start(f32[576,256]{1,0:T(8,128)S(1)} %slice_add_fusion), channel_id=1, source_target_pairs={{0,2},{1,3},{2,0},{3,1},{4,6},{5,7},{6,4},{7,5},{8,10},{9,11},{10,... | collective-permute-start | bytes 1769480 | tf_op jit(solution)/shard_map/ppermute | solution.py:319
  66.4 30.9 %copy-start.5 = (f32[144,256]{1,0:T(8,128)S(1)}, f32[144,256]{1,0:T(8,128)}, u32[]{:S(2)}) copy-start(f32[144,256]{1,0:T(8,128)} %get-tuple-element.46) | copy-start | bytes 442372
  66.5 17.8 %collective-permute-start.14 = (f32[128,256]{1,0:T(8,128)S(1)}, f32[128,256]{1,0:T(8,128)S(1)}, u32[]{:S(2)}, u32[]{:S(2)}) collective-permute-start(f32[128,256]{1,0:T(8,128)S(1)} %slice_add_fusion.11), channel_id=1, source_target_pairs={{0,2},{1,3},{2,0},{3,1},{4,6},{5,7},{6,4},{7,5},{8,10},{9,11},{10,... | collective-permute-start | bytes 393224 | tf_op jit(solution)/shard_map/ppermute | solution.py:319
  68.9 28.6 %copy-start.12 = (f32[64,256]{1,0:T(8,128)S(1)}, f32[64,256]{1,0:T(8,128)}, u32[]{:S(2)}) copy-start(f32[64,256]{1,0:T(8,128)} %get-tuple-element.36) | copy-start | bytes 196612
  68.9 18.7 %collective-permute-start.6 = (f32[128,256]{1,0:T(8,128)S(1)}, f32[128,256]{1,0:T(8,128)S(1)}, u32[]{:S(2)}, u32[]{:S(2)}) collective-permute-start(f32[128,256]{1,0:T(8,128)S(1)} %slice_add_fusion.13), channel_id=1, source_target_pairs={{0,4},{1,5},{2,6},{3,7},{4,0},{5,1},{6,2},{7,3},{8,12},{9,13},{10,... | collective-permute-start | bytes 393224 | tf_op jit(solution)/shard_map/ppermute | solution.py:319
  84.3 21.1 %copy-start.4 = (f32[144,256]{1,0:T(8,128)S(1)}, f32[144,256]{1,0:T(8,128)}, u32[]{:S(2)}) copy-start(f32[144,256]{1,0:T(8,128)} %get-tuple-element.42) | copy-start | bytes 442372
  84.3 6.4 %collective-permute-start.15 = (f32[64,256]{1,0:T(8,128)S(1)}, f32[64,256]{1,0:T(8,128)S(1)}, u32[]{:S(2)}, u32[]{:S(2)}) collective-permute-start(f32[64,256]{1,0:T(8,128)S(1)} %slice_add_fusion.15), channel_id=1, source_target_pairs={{0,8},{1,9},{2,10},{3,11},{4,12},{5,13},{6,14},{7,15},{8,0},{9,1},... | collective-permute-start | bytes 196616 | tf_op jit(solution)/shard_map/ppermute | solution.py:319
  86.1 11.3 %collective-permute-start.10 = (f32[288,256]{1,0:T(8,128)S(1)}, f32[288,256]{1,0:T(8,128)S(1)}, u32[]{:S(2)}, u32[]{:S(2)}) collective-permute-start(f32[288,256]{1,0:T(8,128)S(1)} %slice_add_fusion.1), channel_id=1, source_target_pairs={{0,4},{1,5},{2,6},{3,7},{4,0},{5,1},{6,2},{7,3},{8,12},{9,13},{10,... | collective-permute-start | bytes 884744 | tf_op jit(solution)/shard_map/ppermute | solution.py:319
  87.6 9.9 %collective-permute-start.7 = (f32[64,256]{1,0:T(8,128)S(1)}, f32[64,256]{1,0:T(8,128)S(1)}, u32[]{:S(2)}, u32[]{:S(2)}) collective-permute-start(f32[64,256]{1,0:T(8,128)S(1)} %slice_add_fusion.21), channel_id=1, source_target_pairs={{0,8},{1,9},{2,10},{3,11},{4,12},{5,13},{6,14},{7,15},{8,0},{9,1},... | collective-permute-start | bytes 196616 | tf_op jit(solution)/shard_map/ppermute | solution.py:319
  97.4 8.0 %collective-permute-start.11 = (f32[144,256]{1,0:T(8,128)S(1)}, f32[144,256]{1,0:T(8,128)S(1)}, u32[]{:S(2)}, u32[]{:S(2)}) collective-permute-start(f32[144,256]{1,0:T(8,128)S(1)} %slice_add_fusion.5), channel_id=1, source_target_pairs={{0,8},{1,9},{2,10},{3,11},{4,12},{5,13},{6,14},{7,15},{8,0},{9,1},... | collective-permute-start | bytes 442376 | tf_op jit(solution)/shard_map/ppermute | solution.py:319
  (8 other events, 35.2 us)
